TPU v7x, 256 devices: a whole 4x4x8 slice. The times are simulated.
256 devices in a mesh: frame: 16 (over z, core), row: 16 (over x, y).
Axes of the slice: x: 4, y: 4, z: 8, core: 2. Of those that a mesh axis runs over, the one named last changes fastest.
Arguments:
- video_frames: bfloat16 [32, 2048, 2048], P('frame', 'row'), may hold values from -6 to 6
- split_frames: bfloat16 [32, 2048, 2048], P('frame', 'row'), may hold values from -6 to 6
- dual_frames: bfloat16 [32, 2048, 2048], P('frame', 'row'), may hold values from -6 to 6
- sensor_image: float32 [2048, 2048], P('row'), may hold values from -24 to 24
- kernel_vertical: bfloat16 [2, 768], replicated, may hold values from -0.21875 to 0.21875
- kernel_horizontal: bfloat16 [2, 768], replicated, may hold values from -0.21875 to 0.21875
- shutter_start: int32 [16], replicated, may hold values from 0 to 31, as said below
- shutter_end: int32 [16], replicated, may hold values from 1 to 32
Outputs:
- video_next: bfloat16 [32, 2048, 2048], P('frame', 'row')
- split_next: bfloat16 [32, 2048, 2048], P('frame', 'row')
- dual_next: bfloat16 [32, 2048, 2048], P('frame', 'row')
Inputs may be any that keep to these rules, and one draw needn't show every extreme that they name: For every row band j, shutter_start[j] < shutter_end[j]; row band j holds sensor rows j * 128 to (j + 1) * 128 - 1.
All inputs are finite; a program needn't handle non-finite values.
Results may differ from a plain program's by a relative error of at most 0.0095.
Values may be sent and summed in bfloat16 or wider, within the bound.
A program may use at most 64 MiB of HBM per device.

v0:
```python
import jax
import jax.numpy as jnp
from jax import lax
from jax.sharding import PartitionSpec as P

tau_step = 0.1
rho_weight = 2.0


def from_behind(value, axis, steps):
    count = lax.axis_size(axis)
    leading, last = (max(0, -steps), min(count, count - steps))
    return lax.ppermute(value, axis, [(source, source + steps) for source in range(leading, last)])


def toeplitz_blocks(kernel, block_rows):
    rank_count = kernel.shape[0]
    padded = jnp.pad(kernel, ((0, 0), (block_rows, block_rows)))
    pieces = jnp.stack(
        [padded[:, block_rows * e + 1 : block_rows * e + 2 * block_rows] for e in range(7)], axis=1
    )
    wrapped = jnp.pad(pieces, ((0, 0), (0, 0), (0, 1)))
    tiled = jnp.tile(wrapped, (1, 1, block_rows))
    shaped = tiled[:, :, : block_rows * (2 * block_rows - 1)].reshape(
        rank_count, 7, block_rows, 2 * block_rows - 1
    )
    return shaped[:, :, :, block_rows - 1 : 2 * block_rows - 1]


def columns_pass(blocks, data, adjoint):
    rank_count, frame_count, row_count, width_cols = data.shape
    block_rows = blocks.shape[-1]
    margin = 3 * block_rows
    padded = jnp.pad(data, ((0, 0), (0, 0), (0, 0), (margin, margin)))
    pattern = "rfhnj,rji->fhni" if adjoint else "rfhnj,rij->fhni"
    summed = jnp.zeros((frame_count, row_count, width_cols // block_rows, block_rows), jnp.float32)
    for offset in range(-3, 4):
        begin_col = (3 - offset if adjoint else 3 + offset) * block_rows
        col_view = padded[:, :, :, begin_col : begin_col + width_cols].reshape(
            rank_count, frame_count, row_count, width_cols // block_rows, block_rows
        )
        summed = summed + jnp.einsum(
            pattern, col_view, blocks[:, offset + 3], preferred_element_type=jnp.float32
        )
    return summed.reshape(frame_count, row_count, width_cols)


def window_mask(shutter_start, shutter_end, band_index, frame_ids):
    pick = jnp.arange(shutter_start.shape[0], dtype=jnp.int32) == band_index
    start_value = jnp.sum(jnp.where(pick, shutter_start, 0))
    end_value = jnp.sum(jnp.where(pick, shutter_end, 0))
    return (start_value <= frame_ids) & (frame_ids < end_value)


def masked_total(mask, frames_data):
    return jnp.sum(jnp.where(mask[:, None, None], frames_data.astype(jnp.float32), 0.0), axis=0)


def per_device(
    video_frames,
    split_frames,
    dual_frames,
    sensor_image,
    kernel_vertical,
    kernel_horizontal,
    shutter_start,
    shutter_end,
):
    frame_count, block_rows, sensor_width = video_frames.shape
    rank_count = kernel_vertical.shape[0]
    vertical_blocks = toeplitz_blocks(kernel_vertical, block_rows)
    horizontal_blocks = toeplitz_blocks(kernel_horizontal, block_rows)
    band_index = lax.axis_index("row")
    local_frames = lax.axis_index("frame") * frame_count + jnp.arange(frame_count, dtype=jnp.int32)
    own_mask = window_mask(shutter_start, shutter_end, band_index, local_frames)
    summed = jnp.zeros((rank_count, frame_count, block_rows, sensor_width), jnp.float32)
    for offset in range(-3, 4):
        neighbor = video_frames if offset == 0 else from_behind(video_frames, "row", -offset)
        summed = summed + jnp.einsum(
            "rij,fjw->rfiw",
            vertical_blocks[:, offset + 3],
            neighbor,
            preferred_element_type=jnp.float32,
        )
    rowed = summed.astype(jnp.bfloat16)
    blurred = columns_pass(horizontal_blocks, rowed, False).astype(jnp.bfloat16)
    measured = lax.psum(masked_total(own_mask, blurred).astype(jnp.bfloat16), "frame").astype(
        jnp.float32
    )
    residual = (measured - sensor_image).astype(jnp.bfloat16)
    back_sum = jnp.zeros((rank_count, frame_count, block_rows, sensor_width), jnp.float32)
    masked_own = jnp.where(own_mask[:, None, None], residual[None], jnp.zeros((), jnp.bfloat16))
    for offset in range(-3, 4):
        neighbor = masked_own if offset == 0 else from_behind(masked_own, "row", offset)
        back_sum = back_sum + jnp.einsum(
            "rji,fjw->rfiw",
            vertical_blocks[:, offset + 3],
            neighbor,
            preferred_element_type=jnp.float32,
        )
    back = back_sum.astype(jnp.bfloat16)
    gradient = columns_pass(horizontal_blocks, back, True)
    current = video_frames.astype(jnp.float32)
    dual_value = dual_frames.astype(jnp.float32)
    moved_frames = current - tau_step * (
        gradient + rho_weight * (current - split_frames.astype(jnp.float32) + dual_value)
    )
    shifted = moved_frames + dual_value
    clamped = jnp.maximum(shifted, 0.0)
    return (
        moved_frames.astype(jnp.bfloat16),
        clamped.astype(jnp.bfloat16),
        (shifted - clamped).astype(jnp.bfloat16),
    )


def solution(mesh):
    return jax.shard_map(
        per_device,
        mesh=mesh,
        in_specs=(
            P("frame", "row", None),
            P("frame", "row", None),
            P("frame", "row", None),
            P("row", None),
            P(),
            P(),
            P(),
            P(),
        ),
        out_specs=(P("frame", "row", None), P("frame", "row", None), P("frame", "row", None)),
        check_vma=False,
    )
```

profile of v0, /device:TPU:104, one launch (start us, length us, event | category | flops | bytes accessed | tf_op | source)
XLA Modules:
  0.0 415.3 jit_solution(2680520664731405176)
XLA Ops:
  7.2 1.3 collective-permute-start.4
  8.5 2.4 collective-permute-start.3
  10.9 4.0 collective-permute-start.2
  14.9 8.7 %collective-permute-start.1 = (bf16[2,128,2048]{2,1,0:T(8,128)(2,1)}, bf16[2,128,2048]{2,1,0:T(8,128)(2,1)}, u32[]{:S(2)}, u32[]{:S(2)}) collective-permute-start(bf16[2,128,2048]{2,1,0:T(8,128)(2,1)} %param.8), channel_id=1, source_target_pairs={{0,2},{1,3},{2,4},{3,5},{4,6},{5,7},{6,8},{7,9},{8,10},{9,11},{10,... | collective-permute-start | bytes 3145736 | tf_op jit(solution)/shard_map/ppermute | solution.py:13
  23.5 2.3 collective-permute-start
  25.8 0.8 constant_dynamic-update-slice_fusion.6
  26.6 0.8 constant_dynamic-update-slice_fusion.5
  27.3 0.8 constant_dynamic-update-slice_fusion.4
  28.1 0.8 constant_dynamic-update-slice_fusion.3
  28.8 0.8 constant_dynamic-update-slice_fusion.2
  29.6 0.8 constant_dynamic-update-slice_fusion.1
  30.4 0.7 constant_dynamic-update-slice_fusion
  31.4 0.6 slice.210
  32.0 3.5 reshape.76
  36.5 1.6 slice.218
  38.1 5.1 %reshape.78 = bf16[2,7,128,255]{3,2,0,1:T(8,128)(2,1)} reshape(bf16[2,7,32640]{2,0,1:T(2,128)(2,1)} %slice.218) | data formatting | bytes 1827840 | tf_op jit(solution)/shard_map/reshape | solution.py:24
  43.1 0.6 fusion.121
  43.8 1.2 compare_and_fusion
  45.0 0.7 fusion.45
  45.7 12.8 %collective-permute-start.5 = (bf16[2,128,2048]{2,1,0:T(8,128)(2,1)S(1)}, bf16[2,128,2048]{2,1,0:T(8,128)(2,1)}, u32[]{:S(2)}, u32[]{:S(2)}) collective-permute-start(bf16[2,128,2048]{2,1,0:T(8,128)(2,1)S(1)} %copy-done), channel_id=1, source_target_pairs={{3,0},{4,1},{5,2},{6,3},{7,4},{8,5},{9,6},{10,7},{11,8},{12,9},{13... | collective-permute-start | bytes 3145736 | tf_op jit(solution)/shard_map/ppermute | solution.py:13
  58.6 2.0 fusion.41
  60.6 2.0 fusion.43
  62.5 31.2 %collective-permute-done.2 = bf16[2,128,2048]{2,1,0:T(8,128)(2,1)} collective-permute-done((bf16[2,128,2048]{2,1,0:T(8,128)(2,1)}, bf16[2,128,2048]{2,1,0:T(8,128)(2,1)}, u32[]{:S(2)}, u32[]{:S(2)}) %collective-permute-start.2) | collective-permute-done | bytes 1048608 | tf_op jit(solution)/shard_map/ppermute | solution.py:13
  93.7 2.0 fusion.47
  95.7 2.1 fusion.49
  97.7 4.0 fusion.51
  101.7 4.7 %collective-permute-done.5 = bf16[2,128,2048]{2,1,0:T(8,128)(2,1)} collective-permute-done((bf16[2,128,2048]{2,1,0:T(8,128)(2,1)S(1)}, bf16[2,128,2048]{2,1,0:T(8,128)(2,1)}, u32[]{:S(2)}, u32[]{:S(2)}) %collective-permute-start.5) | collective-permute-done | bytes 1048608 | tf_op jit(solution)/shard_map/ppermute | solution.py:13
  106.5 4.5 %add_convert_fusion.1 = bf16[2,128,2,2048]{3,1,2,0:T(8,128)(2,1)S(1)} fusion(f32[2,128,2,2048]{3,1,2,0:T(8,128)S(1)} %fusion.41, f32[2,128,2,2048]{3,1,2,0:T(8,128)S(1)} %fusion.43, f32[2,128,2,2048]{3,1,2,0:T(8,128)S(1)} %fusion.45, f32[2,128,2,2048]{3,1,2,0:T(8,128)S(1)} %fusion.47, f32[2,128,2,2048]{3,1,2,0:T(8,128)} %fusion.51, ...), kind=kOutput, calls=%fused_computation.1 | convolution fusion | flops 275775488 | bytes 28377088 | tf_op jit(solution)/shard_map/rij,fjw->rfiw/dot_general | solution.py:79
  111.0 1.4 pad_slice_fusion.11
  114.2 1.0 fusion.13
  115.2 1.0 fusion.15
  116.1 0.6 copy.173
  116.8 1.0 fusion.5
  117.7 0.6 copy.172
  118.4 1.0 fusion.7
  119.3 0.6 copy.171
  120.0 1.0 fusion.9
  120.9 0.6 copy.170
  121.5 1.0 fusion.11
  123.1 1.9 select_reduce_fusion
  125.0 1.0 copy.87
  126.8 134.6 %all-reduce.8.cloned.1.call-done = bf16[128,2048]{0,1:T(8,128)(2,1)} async-done(((bf16[128,2048]{0,1:T(8,128)(2,1)}), bf16[128,2048]{0,1:T(8,128)(2,1)}) %all-reduce.8.cloned.1.call-update) | async-done | bytes 524304 | tf_op jit(solution)/shard_map/psum | solution.py:87
  261.4 1.1 subtract_convert_fusion
  262.7 3.4 collective-permute-start.9
  266.1 2.5 collective-permute-start.8
  268.6 1.3 collective-permute-start.7
  269.9 1.3 collective-permute-start.6
  271.2 6.7 %collective-permute-start.10 = (bf16[2,128,2048]{1,2,0:T(8,128)(2,1)S(1)}, bf16[2,128,2048]{1,2,0:T(8,128)(2,1)S(1)}, u32[]{:S(2)}, u32[]{:S(2)}) collective-permute-start(bf16[2,128,2048]{1,2,0:T(8,128)(2,1)S(1)} %broadcast_select_fusion), channel_id=1, source_target_pairs={{0,2},{1,3},{2,4},{3,5},{4,6},{5,7},{6,8},{7,9},{8,10},{9,11},{10,... | collective-permute-start | bytes 3145736 | tf_op jit(solution)/shard_map/ppermute | solution.py:13
  278.0 1.7 fusion.29
  279.6 11.0 %collective-permute-done.9 = bf16[2,128,2048]{1,2,0:T(8,128)(2,1)S(1)} collective-permute-done((bf16[2,128,2048]{1,2,0:T(8,128)(2,1)S(1)}, bf16[2,128,2048]{1,2,0:T(8,128)(2,1)S(1)}, u32[]{:S(2)}, u32[]{:S(2)}) %collective-permute-start.9) | collective-permute-done | bytes 1048608 | tf_op jit(solution)/shard_map/ppermute | solution.py:13
  290.6 16.3 %collective-permute-start.11 = (bf16[2,128,2048]{1,2,0:T(8,128)(2,1)S(1)}, bf16[2,128,2048]{1,2,0:T(8,128)(2,1)}, u32[]{:S(2)}, u32[]{:S(2)}) collective-permute-start(bf16[2,128,2048]{1,2,0:T(8,128)(2,1)S(1)} %broadcast_select_fusion), channel_id=1, source_target_pairs={{0,3},{1,4},{2,5},{3,6},{4,7},{5,8},{6,9},{7,10},{8,11},{9,12},{10... | collective-permute-start | bytes 3145736 | tf_op jit(solution)/shard_map/ppermute | solution.py:13
  306.9 1.7 fusion.27
  308.6 5.8 %collective-permute-done.8 = bf16[2,128,2048]{1,2,0:T(8,128)(2,1)S(1)} collective-permute-done((bf16[2,128,2048]{1,2,0:T(8,128)(2,1)S(1)}, bf16[2,128,2048]{1,2,0:T(8,128)(2,1)S(1)}, u32[]{:S(2)}, u32[]{:S(2)}) %collective-permute-start.8) | collective-permute-done | bytes 1048608 | tf_op jit(solution)/shard_map/ppermute | solution.py:13
  314.4 1.7 fusion.31
  316.0 0.7 collective-permute-done.7
  316.7 1.7 fusion.33
  318.4 62.0 %collective-permute-done.6 = bf16[2,128,2048]{1,2,0:T(8,128)(2,1)S(1)} collective-permute-done((bf16[2,128,2048]{1,2,0:T(8,128)(2,1)S(1)}, bf16[2,128,2048]{1,2,0:T(8,128)(2,1)S(1)}, u32[]{:S(2)}, u32[]{:S(2)}) %collective-permute-start.6) | collective-permute-done | bytes 1048608 | tf_op jit(solution)/shard_map/ppermute | solution.py:13
  380.4 1.7 fusion.35
  382.1 3.6 fusion.25
  385.8 4.9 %add_convert_fusion = bf16[2,2048,2,128]{3,1,2,0:T(8,128)(2,1)S(1)} fusion(f32[2,2048,2,128]{3,1,2,0:T(8,128)} %fusion.25, f32[2,2048,2,128]{3,1,2,0:T(8,128)S(1)} %fusion.27, f32[2,2048,2,128]{3,1,2,0:T(8,128)S(1)} %fusion.29, f32[2,2048,2,128]{3,1,2,0:T(8,128)S(1)} %fusion.31, f32[2,2048,2,128]{3,1,2,0:T(8,128)S(1)} %fusion.35, ...), kind=kOutput, calls=%fused_computation | convolution fusion | flops 275775488 | bytes 28377088 | tf_op jit(solution)/shard_map/rji,fjw->rfiw/dot_general | solution.py:95
  390.7 5.0 %pad_slice_fusion = (bf16[2,2,128,2048]{2,3,0,1:T(8,128)(2,1)S(1)}, bf16[2,2,128,2048]{2,3,0,1:T(8,128)(2,1)S(1)}, bf16[2,2,128,2048]{2,3,0,1:T(8,128)(2,1)S(1)}...) fusion(bf16[2,2,128,2048]{2,3,0,1:T(8,128)(2,1)S(1)} %bitcast.403), kind=kLoop, calls=%fused_computation.2 | loop fusion | bytes 14680064 | tf_op jit(solution)/shard_map/slice | solution.py:39
  399.1 2.7 bitcast_add_fusion
  401.8 1.9 copy.103
  403.7 4.4 %fusion.3 = (bf16[2,128,2048]{2,1,0:T(8,128)(2,1)}, bf16[2,128,2048]{2,1,0:T(8,128)(2,1)}, bf16[2,128,2048]{2,1,0:T(8,128)(2,1)}) fusion(bf16[2,128,2048]{2,1,0:T(8,128)(2,1)} %param.10, f32[2,128,2048]{2,1,0:T(8,128)S(1)} %copy.103, bf16[2,128,2048]{2,1,0:T(8,128)(2,1)} %param.9, bf16[2,128,2048]{2,1,0:T(8,128)(2,1)S(1)} %copy-done), kind=kLoop, calls=%fused_computation.23 | loop fusion | flops 7864320 | bytes 8388608 | tf_op jit(solution)/shard_map/convert_element_type | solution.py:113
  (48 shorter events, 7.8 us)
Async XLA Ops:
  7.2 254.2 %all-reduce.8.cloned.1.call-start = ((), (), s32[]{:S(2)}) async-start(), calls=%async_computation | async-start | bytes 1048576 | tf_op jit(solution)/shard_map/psum | solution.py:87
  7.2 38.5 %collective-permute-start.4 = (bf16[2,128,2048]{2,1,0:T(8,128)(2,1)}, bf16[2,128,2048]{2,1,0:T(8,128)(2,1)}, u32[]{:S(2)}, u32[]{:S(2)}) collective-permute-start(bf16[2,128,2048]{2,1,0:T(8,128)(2,1)} %param.8), channel_id=1, source_target_pairs={{2,0},{3,1},{4,2},{5,3},{6,4},{7,5},{8,6},{9,7},{10,8},{11,9},{12,... | collective-permute-start | bytes 3145736 | tf_op jit(solution)/shard_map/ppermute | solution.py:13
  8.5 52.0 %collective-permute-start.3 = (bf16[2,128,2048]{2,1,0:T(8,128)(2,1)}, bf16[2,128,2048]{2,1,0:T(8,128)(2,1)}, u32[]{:S(2)}, u32[]{:S(2)}) collective-permute-start(bf16[2,128,2048]{2,1,0:T(8,128)(2,1)} %param.8), channel_id=1, source_target_pairs={{1,0},{2,1},{3,2},{4,3},{5,4},{6,5},{7,6},{8,7},{9,8},{10,9},{11,1... | collective-permute-start | bytes 3145736 | tf_op jit(solution)/shard_map/ppermute | solution.py:13
  10.9 82.8 %collective-permute-start.2 = (bf16[2,128,2048]{2,1,0:T(8,128)(2,1)}, bf16[2,128,2048]{2,1,0:T(8,128)(2,1)}, u32[]{:S(2)}, u32[]{:S(2)}) collective-permute-start(bf16[2,128,2048]{2,1,0:T(8,128)(2,1)} %param.8), channel_id=1, source_target_pairs={{0,1},{1,2},{2,3},{3,4},{4,5},{5,6},{6,7},{7,8},{8,9},{9,10},{10,1... | collective-permute-start | bytes 3145736 | tf_op jit(solution)/shard_map/ppermute | solution.py:13
  14.9 80.8 %collective-permute-start.1 = (bf16[2,128,2048]{2,1,0:T(8,128)(2,1)}, bf16[2,128,2048]{2,1,0:T(8,128)(2,1)}, u32[]{:S(2)}, u32[]{:S(2)}) collective-permute-start(bf16[2,128,2048]{2,1,0:T(8,128)(2,1)} %param.8), channel_id=1, source_target_pairs={{0,2},{1,3},{2,4},{3,5},{4,6},{5,7},{6,8},{7,9},{8,10},{9,11},{10,... | collective-permute-start | bytes 3145736 | tf_op jit(solution)/shard_map/ppermute | solution.py:13
  23.5 74.2 %collective-permute-start = (bf16[2,128,2048]{2,1,0:T(8,128)(2,1)}, bf16[2,128,2048]{2,1,0:T(8,128)(2,1)}, u32[]{:S(2)}, u32[]{:S(2)}) collective-permute-start(bf16[2,128,2048]{2,1,0:T(8,128)(2,1)} %param.8), channel_id=1, source_target_pairs={{0,3},{1,4},{2,5},{3,6},{4,7},{5,8},{6,9},{7,10},{8,11},{9,12},{10... | collective-permute-start | bytes 3145736 | tf_op jit(solution)/shard_map/ppermute | solution.py:13
  31.4 4.2 %copy-start.5 = (bf16[2,768]{1,0:T(2,128)(2,1)S(1)}, bf16[2,768]{1,0:T(2,128)(2,1)}, u32[]{:S(2)}) copy-start(bf16[2,768]{1,0:T(2,128)(2,1)} %param.13) | copy-start | bytes 9220
  35.6 58.1 %copy-start.3 = (bf16[2,7,128,255]{3,2,0,1:T(8,128)(2,1)}, bf16[2,7,128,255]{3,2,0,1:T(8,128)(2,1)S(1)}, u32[]{:S(2)}) copy-start(bf16[2,7,128,255]{3,2,0,1:T(8,128)(2,1)S(1)} %reshape.76) | copy-start | bytes 2741764
  36.5 6.6 %copy-start.6 = (s32[16]{0:T(128)S(1)}, s32[16]{0:T(128)}, u32[]{:S(2)}) copy-start(s32[16]{0:T(128)} %param.14) | copy-start | bytes 196
  36.5 6.6 %copy-start.7 = (s32[16]{0:T(128)S(1)}, s32[16]{0:T(128)}, u32[]{:S(2)}) copy-start(s32[16]{0:T(128)} %param.15) | copy-start | bytes 196
  36.5 8.5 %copy-start = (bf16[2,128,2048]{2,1,0:T(8,128)(2,1)S(1)}, bf16[2,128,2048]{2,1,0:T(8,128)(2,1)}, u32[]{:S(2)}) copy-start(bf16[2,128,2048]{2,1,0:T(8,128)(2,1)} %param.8) | copy-start | bytes 3145732
  45.7 60.7 %collective-permute-start.5 = (bf16[2,128,2048]{2,1,0:T(8,128)(2,1)S(1)}, bf16[2,128,2048]{2,1,0:T(8,128)(2,1)}, u32[]{:S(2)}, u32[]{:S(2)}) collective-permute-start(bf16[2,128,2048]{2,1,0:T(8,128)(2,1)S(1)} %copy-done), channel_id=1, source_target_pairs={{3,0},{4,1},{5,2},{6,3},{7,4},{8,5},{9,6},{10,7},{11,8},{12,9},{13... | collective-permute-start | bytes 3145736 | tf_op jit(solution)/shard_map/ppermute | solution.py:13
  113.0 1.2 copy-start.1
  125.0 1.4 copy-start.4
  262.7 27.9 %collective-permute-start.9 = (bf16[2,128,2048]{1,2,0:T(8,128)(2,1)S(1)}, bf16[2,128,2048]{1,2,0:T(8,128)(2,1)S(1)}, u32[]{:S(2)}, u32[]{:S(2)}) collective-permute-start(bf16[2,128,2048]{1,2,0:T(8,128)(2,1)S(1)} %broadcast_select_fusion), channel_id=1, source_target_pairs={{0,1},{1,2},{2,3},{3,4},{4,5},{5,6},{6,7},{7,8},{8,9},{9,10},{10,1... | collective-permute-start | bytes 3145736 | tf_op jit(solution)/shard_map/ppermute | solution.py:13
  266.1 48.3 %collective-permute-start.8 = (bf16[2,128,2048]{1,2,0:T(8,128)(2,1)S(1)}, bf16[2,128,2048]{1,2,0:T(8,128)(2,1)S(1)}, u32[]{:S(2)}, u32[]{:S(2)}) collective-permute-start(bf16[2,128,2048]{1,2,0:T(8,128)(2,1)S(1)} %broadcast_select_fusion), channel_id=1, source_target_pairs={{1,0},{2,1},{3,2},{4,3},{5,4},{6,5},{7,6},{8,7},{9,8},{10,9},{11,1... | collective-permute-start | bytes 3145736 | tf_op jit(solution)/shard_map/ppermute | solution.py:13
  268.6 48.1 %collective-permute-start.7 = (bf16[2,128,2048]{1,2,0:T(8,128)(2,1)S(1)}, bf16[2,128,2048]{1,2,0:T(8,128)(2,1)S(1)}, u32[]{:S(2)}, u32[]{:S(2)}) collective-permute-start(bf16[2,128,2048]{1,2,0:T(8,128)(2,1)S(1)} %broadcast_select_fusion), channel_id=1, source_target_pairs={{2,0},{3,1},{4,2},{5,3},{6,4},{7,5},{8,6},{9,7},{10,8},{11,9},{12,... | collective-permute-start | bytes 3145736 | tf_op jit(solution)/shard_map/ppermute | solution.py:13
  269.9 110.5 %collective-permute-start.6 = (bf16[2,128,2048]{1,2,0:T(8,128)(2,1)S(1)}, bf16[2,128,2048]{1,2,0:T(8,128)(2,1)S(1)}, u32[]{:S(2)}, u32[]{:S(2)}) collective-permute-start(bf16[2,128,2048]{1,2,0:T(8,128)(2,1)S(1)} %broadcast_select_fusion), channel_id=1, source_target_pairs={{3,0},{4,1},{5,2},{6,3},{7,4},{8,5},{9,6},{10,7},{11,8},{12,9},{13... | collective-permute-start | bytes 3145736 | tf_op jit(solution)/shard_map/ppermute | solution.py:13
  271.2 110.9 %collective-permute-start.10 = (bf16[2,128,2048]{1,2,0:T(8,128)(2,1)S(1)}, bf16[2,128,2048]{1,2,0:T(8,128)(2,1)S(1)}, u32[]{:S(2)}, u32[]{:S(2)}) collective-permute-start(bf16[2,128,2048]{1,2,0:T(8,128)(2,1)S(1)} %broadcast_select_fusion), channel_id=1, source_target_pairs={{0,2},{1,3},{2,4},{3,5},{4,6},{5,7},{6,8},{7,9},{8,10},{9,11},{10,... | collective-permute-start | bytes 3145736 | tf_op jit(solution)/shard_map/ppermute | solution.py:13
  290.6 95.1 %collective-permute-start.11 = (bf16[2,128,2048]{1,2,0:T(8,128)(2,1)S(1)}, bf16[2,128,2048]{1,2,0:T(8,128)(2,1)}, u32[]{:S(2)}, u32[]{:S(2)}) collective-permute-start(bf16[2,128,2048]{1,2,0:T(8,128)(2,1)S(1)} %broadcast_select_fusion), channel_id=1, source_target_pairs={{0,3},{1,4},{2,5},{3,6},{4,7},{5,8},{6,9},{7,10},{8,11},{9,12},{10... | collective-permute-start | bytes 3145736 | tf_op jit(solution)/shard_map/ppermute | solution.py:13
  390.7 5.1 %copy-start.2 = (bf16[2,7,128,255]{3,2,0,1:T(8,128)(2,1)S(1)}, bf16[2,7,128,255]{3,2,0,1:T(8,128)(2,1)}, u32[]{:S(2)}) copy-start(bf16[2,7,128,255]{3,2,0,1:T(8,128)(2,1)} %reshape.78) | copy-start | bytes 2741764
Sparse Core Ops, SparseCore 0:
  126.2 135.1 all-reduce.7
where the time goes:
time: 423 us; the launch traced here: 415 us
  waiting for transfers between devices  250 us (59%)
  starting transfers between devices  63 us (15%)
  matrix products  47.8 us (11%)
  local copies, waits for them, and re-layouts  32.1 us (8%)
  between operations  14.9 us (4%)
  other arithmetic  7.48 us (2%)
    psum x1, waiting for transfers between devices, per_device(): lax.psum(masked_total(own_mask, blurred).astype(jnp.bfloat16), 'frame')  135 us
    ppermute x12, waiting for transfers between devices, from_behind(): lax.ppermute(value, axis, [(source, source + steps) for source in range(l...  115 us
    ppermute x12, starting transfers between devices, from_behind(): lax.ppermute(value, axis, [(source, source + steps) for source in range(l...  62.9 us
    dot_general x7, matrix products, per_device(): jnp.einsum('rij,fjw->rfiw', vertical_blocks[:, offset + 3], neighbor, pre...  17.2 us
    dot_general x7, matrix products, per_device(): jnp.einsum('rji,fjw->rfiw', vertical_blocks[:, offset + 3], neighbor, pre...  16.9 us
    dot_general x14, matrix products, columns_pass(): jnp.einsum(pattern, col_view, blocks[:, offset + 3], preferred_element_ty...  13.7 us
    unnamed x36, local copies, waits for them, and re-layouts  10.6 us
    reshape x2, local copies, waits for them, and re-layouts, toeplitz_blocks(): tiled[:, :, :block_rows * (2 * block_rows - 1)]  8.59 us
  transfers between devices with their start and end apart: 13, of which 7 were waited for; matrix products, arithmetic and copies ran while one was open for 11% of the time, Pallas kernels for 0%

commit v1 on v0

v1 whole, which is shorter than its diff:
```python
import functools

import jax
import jax.numpy as jnp
from jax import lax
from jax.experimental import pallas as pl
from jax.experimental.pallas import tpu as pltpu
from jax.sharding import PartitionSpec as P

MESH = pl.DeviceIdType.MESH
tau_step = 0.1
rho_weight = 2.0
REACH = 3
DIAGS = 2 * REACH + 1
F32 = jnp.float32
BF16 = jnp.bfloat16


def dot(a, b, contract):
    return lax.dot_general(a, b, (contract, ((), ())), preferred_element_type=F32)


def wrap(index, count):
    return lax.rem(index + count, count)


def banded(kernel_ref, out_ref, block):
    rank_count, taps = kernel_ref.shape
    padded = jnp.concatenate(
        [kernel_ref[...].astype(F32), jnp.zeros((rank_count, block), F32)], axis=1
    )
    for r in range(rank_count):
        rows = jnp.broadcast_to(padded[r : r + 1], (block, taps + block))
        out_ref[r] = pltpu.roll(rows, 0, 1, stride=1, stride_axis=0).astype(BF16)


def kernel(
    start_ref, end_ref, video_ref, sensor_ref, kv_ref, kh_ref, grad_ref,
    frames_buf, sensor_buf, vert, horiz, sums, t_send, t_recv, p_send, p_recv, res_recv, h_send, h_recv, g_send,
    local_sem, a_send, a_recv, ts_sem, tr_sem, ps_sem, pr_sem, rs_sem, rr_sem, hs_sem, hr_sem, gs_sem, gr_sem,
):
    frame_devices, local_count, block, slice_cols = frames_buf.shape
    bands = start_ref.shape[0]
    rank_count = kv_ref.shape[0]
    me = lax.axis_index("frame")
    band = lax.axis_index("row")
    steps = [d for d in range(-REACH, REACH + 1) if d != 0]

    def frame_peer(d):
        return (wrap(me + d, frame_devices), band)

    def row_peer(d):
        return (me, wrap(band + d, bands))

    def columns(index):
        return pl.ds(pl.multiple_of(index * slice_cols, slice_cols), slice_cols)

    barrier = pltpu.get_barrier_semaphore()

    def greet(k, carry):
        pl.semaphore_signal(barrier, inc=1, device_id=frame_peer(k), device_id_type=MESH)
        return carry

    lax.fori_loop(1, frame_devices, greet, 0)
    for d in steps:
        pl.semaphore_signal(barrier, inc=1, device_id=row_peer(d), device_id_type=MESH)
    pl.semaphore_wait(barrier, frame_devices - 1 + len(steps))

    def a_copy(k):
        target = frame_peer(k)
        return pltpu.make_async_remote_copy(
            src_ref=video_ref.at[:, :, columns(target[0])],
            dst_ref=frames_buf.at[me],
            send_sem=a_send.at[k],
            recv_sem=a_recv.at[k],
            device_id=target,
            device_id_type=MESH,
        )

    def start_a(k, carry):
        a_copy(k).start()
        return carry

    lax.fori_loop(1, frame_devices, start_a, 0)
    own_copy = pltpu.make_async_copy(
        video_ref.at[:, :, columns(me)], frames_buf.at[me], local_sem.at[0]
    )
    own_copy.start()
    sensor_copy = pltpu.make_async_copy(sensor_ref.at[:, columns(me)], sensor_buf, local_sem.at[1])
    sensor_copy.start()

    banded(kv_ref, vert, block)
    banded(kh_ref, horiz, block)

    def on(frame, band_index):
        inside = (band_index >= 0) & (band_index < bands)
        at = jnp.clip(band_index, 0, bands - 1)
        active = inside & (start_ref[at] <= frame) & (frame < end_ref[at])
        return jnp.where(active, 1.0, 0.0).astype(F32)

    def add_frames(source, first):
        for d in range(-REACH, REACH + 1):
            total = None if first else sums[d + REACH]
            for i in range(local_count):
                term = frames_buf[source, i].astype(F32) * on(source * local_count + i, band + d)
                total = term if total is None else total + term
            sums[d + REACH] = total

    own_copy.wait()
    add_frames(me, True)

    def arrive(k, carry):
        a_copy(k).wait_recv()
        add_frames(wrap(me - k, frame_devices), False)
        return carry

    lax.fori_loop(1, frame_devices, arrive, 0)

    def send(src, dst, send_sem, recv_sem, target):
        copy = pltpu.make_async_remote_copy(
            src_ref=src, dst_ref=dst, send_sem=send_sem, recv_sem=recv_sem,
            device_id=target, device_id_type=MESH,
        )
        copy.start()
        return copy

    def kept(value, index, count):
        return value * jnp.where((index >= 0) & (index < count), 1.0, 0.0).astype(value.dtype)

    t_copies = []
    for d in steps:
        t_send[d + REACH] = sums[d + REACH].astype(BF16)
        t_copies.append(
            send(t_send.at[d + REACH], t_recv.at[REACH - d], ts_sem.at[d + REACH], tr_sem.at[REACH - d], row_peer(d))
        )
    t_recv[REACH] = sums[REACH].astype(BF16)
    for copy in t_copies:
        copy.wait()
    window = jnp.concatenate(
        [kept(t_recv[d + REACH], band + d, bands) for d in range(-REACH, REACH + 1)], axis=0
    )
    rowed = [dot(vert[r], window, ((1,), (0,))).astype(BF16) for r in range(rank_count)]

    def part(d):
        total = None
        for r in range(rank_count):
            block_d = horiz[r, :, (d + REACH) * block : (d + REACH + 1) * block]
            term = dot(rowed[r], block_d, ((1,), (1,)))
            total = term if total is None else total + term
        return total

    p_copies = []
    for d in steps:
        p_send[d + REACH] = part(d).astype(BF16)
        p_copies.append(
            send(p_send.at[d + REACH], p_recv.at[d + REACH], ps_sem.at[d + REACH], pr_sem.at[d + REACH], frame_peer(-d))
        )
    measured = part(0)
    for copy in p_copies:
        copy.wait()
    for d in steps:
        measured = measured + kept(p_recv[d + REACH].astype(F32), me + d, frame_devices)
    sensor_copy.wait()
    residual = (measured - sensor_buf[...]).astype(BF16)

    res_recv[REACH] = residual
    r_copies = [
        send(res_recv.at[REACH], res_recv.at[d + REACH], rs_sem.at[d + REACH], rr_sem.at[d + REACH], frame_peer(d))
        for d in steps
    ]
    for copy in r_copies:
        copy.wait()
    pieces = [kept(res_recv[d + REACH], me - d, frame_devices) for d in range(-REACH, REACH + 1)]
    spread = []
    for r in range(rank_count):
        total = None
        for d in range(-REACH, REACH + 1):
            block_d = horiz[r, :, (d + REACH) * block : (d + REACH + 1) * block]
            term = dot(pieces[d + REACH], block_d, ((1,), (0,)))
            total = term if total is None else total + term
        spread.append(total.astype(BF16))

    def back(d):
        total = None
        for r in range(rank_count):
            block_d = vert[r, :, (d + REACH) * block : (d + REACH + 1) * block]
            term = dot(block_d, spread[r], ((0,), (0,)))
            total = term if total is None else total + term
        return total.astype(BF16)

    h_copies = []
    for d in steps:
        h_send[d + REACH] = back(d)
        h_copies.append(
            send(h_send.at[d + REACH], h_recv.at[d + REACH], hs_sem.at[d + REACH], hr_sem.at[d + REACH], row_peer(d))
        )
    h_recv[REACH] = back(0)
    for copy in h_copies:
        copy.wait()

    def gradients(target):
        for i in range(local_count):
            total = None
            for d in range(-REACH, REACH + 1):
                term = h_recv[d + REACH].astype(F32) * on(target * local_count + i, band - d)
                total = term if total is None else total + term
            g_send[target, i] = total.astype(BF16)

    def g_copy(k):
        target = frame_peer(k)
        return pltpu.make_async_remote_copy(
            src_ref=g_send.at[target[0]],
            dst_ref=grad_ref.at[:, :, columns(me)],
            send_sem=gs_sem.at[k],
            recv_sem=gr_sem.at[k],
            device_id=target,
            device_id_type=MESH,
        )

    def give(k, carry):
        gradients(wrap(me + k, frame_devices))
        g_copy(k).start()
        return carry

    lax.fori_loop(1, frame_devices, give, 0)
    gradients(me)
    own_grad = pltpu.make_async_copy(g_send.at[me], grad_ref.at[:, :, columns(me)], local_sem.at[0])
    own_grad.start()

    def finish(k, carry):
        a_copy(k).wait_send()
        g_copy(k).wait()
        return carry

    lax.fori_loop(1, frame_devices, finish, 0)
    own_grad.wait()


def per_device(
    video_frames, split_frames, dual_frames, sensor_image, kernel_vertical, kernel_horizontal, shutter_start, shutter_end
):
    local_count, block, width = video_frames.shape
    rank_count, taps = kernel_vertical.shape
    frame_devices = lax.axis_size("frame")
    slice_cols = width // frame_devices
    smem = pl.BlockSpec(memory_space=pltpu.SMEM)
    vmem = pl.BlockSpec(memory_space=pltpu.VMEM)
    anywhere = pl.BlockSpec(memory_space=pl.ANY)
    dma = pltpu.SemaphoreType.DMA
    tile = (block, slice_cols)
    gradient = pl.pallas_call(
        kernel,
        out_shape=jax.ShapeDtypeStruct((local_count, block, width), BF16),
        in_specs=[smem, smem, anywhere, anywhere, vmem, vmem],
        out_specs=anywhere,
        scratch_shapes=[
            pltpu.VMEM((frame_devices, local_count) + tile, BF16),
            pltpu.VMEM(tile, F32),
            pltpu.VMEM((rank_count, block, taps + block), BF16),
            pltpu.VMEM((rank_count, block, taps + block), BF16),
            pltpu.VMEM((DIAGS,) + tile, F32),
        ]
        + [pltpu.VMEM((DIAGS,) + tile, BF16)] * 7
        + [pltpu.VMEM((frame_devices, local_count) + tile, BF16)]
        + [dma((2,)), dma((frame_devices,)), dma((frame_devices,))]
        + [dma((DIAGS,))] * 8
        + [dma((frame_devices,)), dma((frame_devices,))],
        compiler_params=pltpu.CompilerParams(
            collective_id=0, has_side_effects=True, vmem_limit_bytes=32 << 20
        ),
        name="blur_and_adjoint",
    )(shutter_start, shutter_end, video_frames, sensor_image, kernel_vertical, kernel_horizontal)
    current = video_frames.astype(F32)
    dual_value = dual_frames.astype(F32)
    moved_frames = current - tau_step * (
        gradient.astype(F32) + rho_weight * (current - split_frames.astype(F32) + dual_value)
    )
    shifted = moved_frames + dual_value
    clamped = jnp.maximum(shifted, 0.0)
    return (
        moved_frames.astype(BF16),
        clamped.astype(BF16),
        (shifted - clamped).astype(BF16),
    )


def solution(mesh):
    frames = P("frame", "row", None)
    return jax.shard_map(
        per_device,
        mesh=mesh,
        in_specs=(frames, frames, frames, P("row", None), P(), P(), P(), P()),
        out_specs=(frames, frames, frames),
        check_vma=False,
    )
```

time: 423 us -> 91 us (0.22)
  the two profiles are of different devices: /device:TPU:104 before, /device:TPU:1 now
where the time goes in v1:
time: 91 us; the launch traced here: 90.8 us
  Pallas kernels  82.2 us (90%)
  local copies, waits for them, and re-layouts  5.13 us (6%)
  other arithmetic  2.77 us (3%)
    pallas_call x1, Pallas kernels, per_device(): pl.pallas_call(kernel, out_shape=jax.ShapeDtypeStruct((local_count, block...  82.2 us
    unnamed x16, local copies, waits for them, and re-layouts  5.13 us
    convert_element_type x1, other arithmetic, per_device(): (shifted - clamped).astype(BF16)  2.77 us

profile of v1, /device:TPU:1, one launch (start us, length us, event | category | flops | bytes accessed | tf_op | source)
XLA Modules:
  0.0 90.8 jit_solution(14159872044522941585)
XLA Ops:
  0.6 0.0 copy-start
  0.6 1.2 %copy-done = bf16[2,128,2048]{2,1,0:T(8,128)(2,1)S(1)} copy-done((bf16[2,128,2048]{2,1,0:T(8,128)(2,1)S(1)}, bf16[2,128,2048]{2,1,0:T(8,128)(2,1)}, u32[]{:S(2)}) %copy-start) | copy-done | bytes 1048600
  1.9 0.0 copy-start.1
  1.9 1.2 %copy-done.1 = f32[128,2048]{1,0:T(8,128)S(1)} copy-done((f32[128,2048]{1,0:T(8,128)S(1)}, f32[128,2048]{1,0:T(8,128)}, u32[]{:S(2)}) %copy-start.1) | copy-done | bytes 1048600
  3.1 0.0 copy-start.2
  3.1 0.7 copy-done.2
  3.8 0.0 copy-start.3
  3.8 0.7 copy-done.3
  4.5 0.0 copy-start.4
  4.5 0.7 copy-done.4
  5.1 0.0 copy-start.5
  5.1 0.7 copy-done.5
  5.8 0.0 copy-start.6
  5.8 0.0 copy-start.7
  5.8 82.2 %blur_and_adjoint.1 = bf16[2,128,2048]{2,1,0:T(8,128)(2,1)S(1)} custom-call(s32[16]{0:T(128)S(1)} %copy-done.4, s32[16]{0:T(128)S(1)} %copy-done.5, bf16[2,128,2048]{2,1,0:T(8,128)(2,1)S(1)} %copy-done, f32[128,2048]{1,0:T(8,128)S(1)} %copy-done.1, bf16[2,768]{1,0:T(2,128)(2,1)S(1)} %copy-done.2, bf16[2,768]{1,0:T(2,128)(2,1)S(1)} %copy-done.3), custom_call_target="tpu_custom_call" | custom-call | tf_op jit(solution)/shard_map/blur_and_adjoint/pallas_call | solution.py:251
  88.0 0.0 copy-done.6
  88.0 0.0 copy-done.7
  88.0 2.8 %fusion.3 = (bf16[2,128,2048]{2,1,0:T(8,128)(2,1)}, bf16[2,128,2048]{2,1,0:T(8,128)(2,1)}, bf16[2,128,2048]{2,1,0:T(8,128)(2,1)}) fusion(bf16[2,128,2048]{2,1,0:T(8,128)(2,1)S(1)} %copy-done.6, bf16[2,128,2048]{2,1,0:T(8,128)(2,1)S(1)} %copy-done.7, bf16[2,128,2048]{2,1,0:T(8,128)(2,1)S(1)} %blur_and_adjoint.1, bf16[2,128,2048]{2,1,0:T(8,128)(2,1)S(1)} %copy-done), kind=kLoop, calls=%fused_computation.9 | loop fusion | flops 8388608 | bytes 7340032 | tf_op jit(solution)/shard_map/convert_element_type | solution.py:283
Async XLA Ops:
  0.6 1.2 %copy-start = (bf16[2,128,2048]{2,1,0:T(8,128)(2,1)S(1)}, bf16[2,128,2048]{2,1,0:T(8,128)(2,1)}, u32[]{:S(2)}) copy-start(bf16[2,128,2048]{2,1,0:T(8,128)(2,1)} %video_ref.1) | copy-start | bytes 3145732
  1.9 1.2 %copy-start.1 = (f32[128,2048]{1,0:T(8,128)S(1)}, f32[128,2048]{1,0:T(8,128)}, u32[]{:S(2)}) copy-start(f32[128,2048]{1,0:T(8,128)} %sensor_ref.1) | copy-start | bytes 3145732
  3.1 0.7 copy-start.2
  3.8 0.7 copy-start.3
  4.5 0.7 copy-start.4
  5.1 0.7 copy-start.5
  5.8 82.3 %copy-start.6 = (bf16[2,128,2048]{2,1,0:T(8,128)(2,1)S(1)}, bf16[2,128,2048]{2,1,0:T(8,128)(2,1)}, u32[]{:S(2)}) copy-start(bf16[2,128,2048]{2,1,0:T(8,128)(2,1)} %param.10) | copy-start | bytes 3145732
  5.8 82.3 %copy-start.7 = (bf16[2,128,2048]{2,1,0:T(8,128)(2,1)S(1)}, bf16[2,128,2048]{2,1,0:T(8,128)(2,1)}, u32[]{:S(2)}) copy-start(bf16[2,128,2048]{2,1,0:T(8,128)(2,1)} %param.9) | copy-start | bytes 3145732

commit v2 on v1

--- a/solution.py
+++ b/solution.py
@@ -35,8 +35,8 @@
 
 
 def kernel(
-    start_ref, end_ref, video_ref, sensor_ref, kv_ref, kh_ref, grad_ref,
-    frames_buf, sensor_buf, vert, horiz, sums, t_send, t_recv, p_send, p_recv, res_recv, h_send, h_recv, g_send,
+    start_hbm, end_hbm, video_ref, sensor_ref, kv_hbm, kh_hbm, grad_ref,
+    start_ref, end_ref, kv_ref, kh_ref, frames_buf, sensor_buf, vert, horiz, sums, t_send, t_recv, p_send, p_recv, res_recv, h_send, h_recv, g_send,
     local_sem, a_send, a_recv, ts_sem, tr_sem, ps_sem, pr_sem, rs_sem, rr_sem, hs_sem, hr_sem, gs_sem, gr_sem,
 ):
     frame_devices, local_count, block, slice_cols = frames_buf.shape
@@ -55,6 +55,14 @@
     def columns(index):
         return pl.ds(pl.multiple_of(index * slice_cols, slice_cols), slice_cols)
 
+    small = [
+        pltpu.make_async_copy(src, dst, local_sem.at[2 + i])
+        for i, (src, dst) in enumerate(
+            [(start_hbm, start_ref), (end_hbm, end_ref), (kv_hbm, kv_ref), (kh_hbm, kh_ref)]
+        )
+    ]
+    for copy in small:
+        copy.start()
     barrier = pltpu.get_barrier_semaphore()
 
     def greet(k, carry):
@@ -88,6 +96,8 @@
     own_copy.start()
     sensor_copy = pltpu.make_async_copy(sensor_ref.at[:, columns(me)], sensor_buf, local_sem.at[1])
     sensor_copy.start()
+    for copy in small:
+        copy.wait()
 
     banded(kv_ref, vert, block)
     banded(kh_ref, horiz, block)
@@ -116,12 +126,15 @@
 
     lax.fori_loop(1, frame_devices, arrive, 0)
 
+    sent = []
+
     def send(src, dst, send_sem, recv_sem, target):
         copy = pltpu.make_async_remote_copy(
             src_ref=src, dst_ref=dst, send_sem=send_sem, recv_sem=recv_sem,
             device_id=target, device_id_type=MESH,
         )
         copy.start()
+        sent.append(copy)
         return copy
 
     def kept(value, index, count):
@@ -135,7 +148,7 @@
         )
     t_recv[REACH] = sums[REACH].astype(BF16)
     for copy in t_copies:
-        copy.wait()
+        copy.wait_recv()
     window = jnp.concatenate(
         [kept(t_recv[d + REACH], band + d, bands) for d in range(-REACH, REACH + 1)], axis=0
     )
@@ -157,7 +170,7 @@
         )
     measured = part(0)
     for copy in p_copies:
-        copy.wait()
+        copy.wait_recv()
     for d in steps:
         measured = measured + kept(p_recv[d + REACH].astype(F32), me + d, frame_devices)
     sensor_copy.wait()
@@ -169,7 +182,7 @@
         for d in steps
     ]
     for copy in r_copies:
-        copy.wait()
+        copy.wait_recv()
     pieces = [kept(res_recv[d + REACH], me - d, frame_devices) for d in range(-REACH, REACH + 1)]
     spread = []
     for r in range(rank_count):
@@ -196,7 +209,7 @@
         )
     h_recv[REACH] = back(0)
     for copy in h_copies:
-        copy.wait()
+        copy.wait_recv()
 
     def gradients(target):
         for i in range(local_count):
@@ -234,6 +247,8 @@
 
     lax.fori_loop(1, frame_devices, finish, 0)
     own_grad.wait()
+    for copy in sent:
+        copy.wait_send()
 
 
 def per_device(
@@ -243,17 +258,21 @@
     rank_count, taps = kernel_vertical.shape
     frame_devices = lax.axis_size("frame")
     slice_cols = width // frame_devices
-    smem = pl.BlockSpec(memory_space=pltpu.SMEM)
-    vmem = pl.BlockSpec(memory_space=pltpu.VMEM)
+    hbm = pl.BlockSpec(memory_space=pltpu.HBM)
     anywhere = pl.BlockSpec(memory_space=pl.ANY)
     dma = pltpu.SemaphoreType.DMA
     tile = (block, slice_cols)
+    operands = (shutter_start, shutter_end, video_frames, sensor_image, kernel_vertical, kernel_horizontal)
     gradient = pl.pallas_call(
         kernel,
         out_shape=jax.ShapeDtypeStruct((local_count, block, width), BF16),
-        in_specs=[smem, smem, anywhere, anywhere, vmem, vmem],
+        in_specs=[hbm] * 6,
         out_specs=anywhere,
         scratch_shapes=[
+            pltpu.SMEM(shutter_start.shape, jnp.int32),
+            pltpu.SMEM(shutter_end.shape, jnp.int32),
+            pltpu.VMEM((rank_count, taps), BF16),
+            pltpu.VMEM((rank_count, taps), BF16),
             pltpu.VMEM((frame_devices, local_count) + tile, BF16),
             pltpu.VMEM(tile, F32),
             pltpu.VMEM((rank_count, block, taps + block), BF16),
@@ -262,14 +281,14 @@
         ]
         + [pltpu.VMEM((DIAGS,) + tile, BF16)] * 7
         + [pltpu.VMEM((frame_devices, local_count) + tile, BF16)]
-        + [dma((2,)), dma((frame_devices,)), dma((frame_devices,))]
+        + [dma((6,)), dma((frame_devices,)), dma((frame_devices,))]
         + [dma((DIAGS,))] * 8
         + [dma((frame_devices,)), dma((frame_devices,))],
         compiler_params=pltpu.CompilerParams(
             collective_id=0, has_side_effects=True, vmem_limit_bytes=32 << 20
         ),
         name="blur_and_adjoint",
-    )(shutter_start, shutter_end, video_frames, sensor_image, kernel_vertical, kernel_horizontal)
+    )(*[pltpu.with_memory_space_constraint(x, pltpu.HBM) for x in operands])
     current = video_frames.astype(F32)
     dual_value = dual_frames.astype(F32)
     moved_frames = current - tau_step * (

time: 91 us -> 85.8 us (0.943)
  local copies, waits for them, and re-layouts: 5.13 us -> 0.01 us
    unnamed x16 -> x6, local copies, waits for them, and re-layouts: 5.13 us -> 0.01 us
where the time goes in v2:
time: 85.8 us; the launch traced here: 85.6 us
  Pallas kernels  82.1 us (96%)
  other arithmetic  2.8 us (3%)
    pallas_call x1, Pallas kernels, per_device(): pl.pallas_call(kernel, out_shape=jax.ShapeDtypeStruct((local_count, block...  82.1 us
    convert_element_type x1, other arithmetic, per_device(): (shifted - clamped).astype(BF16)  2.8 us

profile of v2, /device:TPU:1, one launch (start us, length us, event | category | flops | bytes accessed | tf_op | source)
XLA Modules:
  0.0 85.6 jit_solution(10441828772884342129)
XLA Ops:
  0.6 0.0 copy-start
  0.6 0.0 copy-start.1
  0.7 0.0 copy-start.2
  0.7 82.1 %blur_and_adjoint.1 = bf16[2,128,2048]{2,1,0:T(8,128)(2,1)S(1)} custom-call(s32[16]{0:T(128)} %start_hbm.1, s32[16]{0:T(128)} %end_hbm.1, bf16[2,128,2048]{2,1,0:T(8,128)(2,1)} %video_ref.1, f32[128,2048]{1,0:T(8,128)} %sensor_ref.1, bf16[2,768]{1,0:T(2,128)(2,1)} %kv_hbm.1, bf16[2,768]{1,0:T(2,128)(2,1)} %kh_hbm.1), custom_call_target="tpu_custom_call" | custom-call | tf_op jit(solution)/shard_map/blur_and_adjoint/pallas_call | solution.py:266
  82.8 0.0 copy-done
  82.8 0.0 copy-done.1
  82.8 0.0 copy-done.2
  82.8 2.8 %fusion.3 = (bf16[2,128,2048]{2,1,0:T(8,128)(2,1)}, bf16[2,128,2048]{2,1,0:T(8,128)(2,1)}, bf16[2,128,2048]{2,1,0:T(8,128)(2,1)}) fusion(bf16[2,128,2048]{2,1,0:T(8,128)(2,1)S(1)} %copy-done.1, bf16[2,128,2048]{2,1,0:T(8,128)(2,1)S(1)} %copy-done.2, bf16[2,128,2048]{2,1,0:T(8,128)(2,1)S(1)} %blur_and_adjoint.1, bf16[2,128,2048]{2,1,0:T(8,128)(2,1)S(1)} %copy-done), kind=kLoop, calls=%fused_computation.9 | loop fusion | flops 8388608 | bytes 7340032 | tf_op jit(solution)/shard_map/convert_element_type | solution.py:302
Async XLA Ops:
  0.6 82.2 %copy-start = (bf16[2,128,2048]{2,1,0:T(8,128)(2,1)S(1)}, bf16[2,128,2048]{2,1,0:T(8,128)(2,1)}, u32[]{:S(2)}) copy-start(bf16[2,128,2048]{2,1,0:T(8,128)(2,1)} %video_ref.1) | copy-start | bytes 3145732
  0.6 82.2 %copy-start.1 = (bf16[2,128,2048]{2,1,0:T(8,128)(2,1)S(1)}, bf16[2,128,2048]{2,1,0:T(8,128)(2,1)}, u32[]{:S(2)}) copy-start(bf16[2,128,2048]{2,1,0:T(8,128)(2,1)} %param.10) | copy-start | bytes 3145732
  0.7 82.2 %copy-start.2 = (bf16[2,128,2048]{2,1,0:T(8,128)(2,1)S(1)}, bf16[2,128,2048]{2,1,0:T(8,128)(2,1)}, u32[]{:S(2)}) copy-start(bf16[2,128,2048]{2,1,0:T(8,128)(2,1)} %param.9) | copy-start | bytes 3145732

commit v3 on v2

v3 whole, which is shorter than its diff:
```python
import functools

import jax
import jax.numpy as jnp
from jax import lax
from jax.experimental import pallas as pl
from jax.experimental.pallas import tpu as pltpu
from jax.sharding import PartitionSpec as P

MESH = pl.DeviceIdType.MESH
tau_step = 0.1
rho_weight = 2.0
REACH = 3
DIAGS = 2 * REACH + 1
F32 = jnp.float32
BF16 = jnp.bfloat16


def dot(a, b, contract):
    return lax.dot_general(a, b, (contract, ((), ())), preferred_element_type=F32)


def wrap(index, count):
    return lax.rem(index + count, count)


def banded(kernel_ref, out_ref, block):
    rank_count, taps = kernel_ref.shape
    padded = jnp.concatenate(
        [kernel_ref[...].astype(F32), jnp.zeros((rank_count, block), F32)], axis=1
    )
    for r in range(rank_count):
        rows = jnp.broadcast_to(padded[r : r + 1], (block, taps + block))
        out_ref[r] = pltpu.roll(rows, 0, 1, stride=1, stride_axis=0).astype(BF16)


def kernel(
    start_hbm, end_hbm, video_ref, sensor_ref, kv_hbm, kh_hbm, grad_ref,
    start_ref, end_ref, kv_ref, kh_ref, sensor_buf, vert, horiz, sums, rowed_ref, spread,
    frames_buf, own_buf, swap_buf, tb_send, tb_recv, part_send, part_recv, t_send, t_recv,
    p_send, p_recv, res_recv, h_send, h_recv, q_recv, hb_send, hb_recv, g_send, gb_send,
    local_sem, own_sem, sw_s, sw_r, a_s, a_r, tb_s, tb_r, part_s, part_r, t_s, t_r,
    p_s, p_r, r_s, r_r, h_s, h_r, q_s, q_r, hb_s, hb_r, g_s, g_r, gb_s, gb_r,
):
    frame_devices, local_count, block, slice_cols = frames_buf.shape
    chips = frame_devices // 2
    shares = chips // 2
    bands = start_ref.shape[0]
    rank_count = kv_ref.shape[0]
    me = lax.axis_index("frame")
    band = lax.axis_index("row")
    chip = me // 2
    core = lax.rem(me, 2)
    sibling = me + 1 - 2 * core
    skew = lax.rem(core + chip, 2)
    steps = [2, -2, 3, -3, 1, -1]
    diagonals = range(-REACH, REACH + 1)

    def frame_peer(d):
        return (wrap(me + d, frame_devices), band)

    def row_peer(d):
        return (me, wrap(band + d, bands))

    def columns(index):
        return pl.ds(pl.multiple_of(index * slice_cols, slice_cols), slice_cols)

    def odd_chip(i):
        return lax.rem(chip + skew + 2 * i, chips)

    def remote(src, dst, send_sem, recv_sem, target):
        return pltpu.make_async_remote_copy(
            src_ref=src, dst_ref=dst, send_sem=send_sem, recv_sem=recv_sem,
            device_id=target, device_id_type=MESH,
        )

    small = [
        pltpu.make_async_copy(src, dst, local_sem.at[2 + i])
        for i, (src, dst) in enumerate(
            [(start_hbm, start_ref), (end_hbm, end_ref), (kv_hbm, kv_ref), (kh_hbm, kh_ref)]
        )
    ]
    for copy in small:
        copy.start()
    own_copies = [
        pltpu.make_async_copy(video_ref.at[:, :, columns(2 * odd_chip(i) + 1)], own_buf.at[i], own_sem.at[i])
        for i in range(shares)
    ]
    for copy in own_copies:
        copy.start()
    own_even = pltpu.make_async_copy(video_ref.at[:, :, columns(2 * chip)], frames_buf.at[me], local_sem.at[0])
    sensor_copy = pltpu.make_async_copy(sensor_ref.at[:, columns(me)], sensor_buf, local_sem.at[1])
    sensor_copy.start()

    @pl.when(core == 0)
    def _():
        own_even.start()

    barrier = pltpu.get_barrier_semaphore()

    def greet(k, carry):
        pl.semaphore_signal(barrier, inc=1, device_id=frame_peer(k), device_id_type=MESH)
        return carry

    lax.fori_loop(1, frame_devices, greet, 0)
    for d in steps:
        pl.semaphore_signal(barrier, inc=1, device_id=row_peer(d), device_id_type=MESH)
    pl.semaphore_wait(barrier, frame_devices - 1 + len(steps))

    def swap_copy(i):
        index = 2 * lax.rem(chip + 1 - skew + 2 * i, chips) + 1
        return remote(video_ref.at[:, :, columns(index)], swap_buf.at[i], sw_s.at[i], sw_r.at[i], (sibling, band))

    def even_copy(k):
        target = 2 * lax.rem(chip + k, chips)
        return remote(
            video_ref.at[:, :, columns(target)], frames_buf.at[me], a_s.at[k], a_r.at[2 * k + core], (target, band)
        )

    order_b = [2, 1, 3, 0]
    for i in order_b:
        swap_copy(i).start()

    def start_even(k, carry):
        even_copy(k).start()
        return carry

    lax.fori_loop(1, chips, start_even, 0)

    @pl.when(core == 1)
    def _():
        even_copy(0).start()

    for copy in small:
        copy.wait()
    banded(kv_ref, vert, block)
    banded(kh_ref, horiz, block)

    def on(frame, band_index):
        inside = (band_index >= 0) & (band_index < bands)
        at = jnp.clip(band_index, 0, bands - 1)
        active = inside & (start_ref[at] <= frame) & (frame < end_ref[at])
        return jnp.where(active, 1.0, 0.0).astype(F32)

    def kept(value, index, count):
        return value * jnp.where((index >= 0) & (index < count), 1.0, 0.0).astype(value.dtype)

    def weighted(pairs):
        total = None
        for value, weight in pairs:
            total = value * weight if total is None else total + value * weight
        return total

    def tb_copy(i, d):
        return remote(
            tb_send.at[i, d + REACH], tb_recv.at[i, REACH - d], tb_s.at[i, d + REACH], tb_r.at[i, REACH - d], row_peer(d)
        )

    def tb_arrival(i, d):
        return remote(tb_send.at[i, d + REACH], tb_recv.at[i, d + REACH], tb_s.at[i, d + REACH], tb_r.at[i, d + REACH], row_peer(d))

    half = block // 4
    for i in order_b:
        own_copies[i].wait()
        swap_copy(i).wait_recv()

        def mix(c, carry):
            part = pl.ds(pl.multiple_of(c * half, half), half)
            mine = [(own_buf[i, f, part].astype(F32), me * local_count + f) for f in range(local_count)]
            others = [(swap_buf[i, f, part].astype(F32), sibling * local_count + f) for f in range(local_count)]
            for d in diagonals:
                total = weighted([(value, on(frame, band + d)) for value, frame in mine + others]).astype(BF16)
                if d == 0:
                    tb_recv[i, REACH, part] = total
                else:
                    tb_send[i, d + REACH, part] = total
            return carry

        lax.fori_loop(0, 4, mix, 0)
        for d in steps:
            tb_copy(i, d).start()

    def add_frames(source, first):
        for d in diagonals:
            total = None if first else sums[d + REACH]
            for f in range(local_count):
                term = frames_buf[source, f].astype(F32) * on(source * local_count + f, band + d)
                total = term if total is None else total + term
            sums[d + REACH] = total

    def even_arrival(k, from_core):
        source = 2 * wrap(chip - k, chips) + from_core
        remote(frames_buf.at[source], frames_buf.at[source], a_s.at[k], a_r.at[2 * k + from_core], (sibling, band)).wait_recv()
        add_frames(source, False)

    def gather_even(low, high):
        def take(q, carry):
            k = wrap(((q + 1) // 2) * (2 * lax.rem(q, 2) - 1), chips)
            even_arrival(k, 0)
            even_arrival(k, 1)
            return carry

        lax.fori_loop(low, high, take, 0)

    def t_copy(d):
        return remote(
            t_send.at[d + REACH], t_recv.at[REACH - d], t_s.at[d + REACH], t_r.at[REACH - d], row_peer(d)
        )

    def t_arrival(d):
        return remote(t_send.at[d + REACH], t_recv.at[d + REACH], t_s.at[d + REACH], t_r.at[d + REACH], row_peer(d))

    def vertical(window_ref, store):
        window = jnp.concatenate([kept(window_ref[d + REACH], band + d, bands) for d in diagonals], axis=0)
        for r in range(rank_count):
            store[r] = dot(vert[r], window, ((1,), (0,))).astype(BF16)

    def part_copy(i):
        owner = 2 * odd_chip(i) + 1
        k = skew + 2 * i
        return remote(part_send.at[i], part_recv.at[k], part_s.at[i], part_r.at[k], (owner, band))

    own_share = (core == 1) & (skew == 0)

    for position, i in enumerate(order_b):
        for d in steps:
            tb_arrival(i, d).wait_recv()
        vertical(tb_recv.at[i], part_send.at[i])
        if i == 0:

            @pl.when(own_share)
            def _():
                part_recv[0] = part_send[0]

            @pl.when(jnp.logical_not(own_share))
            def _():
                part_copy(0).start()

        else:
            part_copy(i).start()

        @pl.when(core == 0)
        def _():
            if position == 0:
                own_even.wait()
                add_frames(me, True)
                even_arrival(0, 1)
                gather_even(1, 3)
            if position == 1:
                gather_even(3, 5)
            if position == 2:
                gather_even(5, chips)
                for d in steps:
                    t_send[d + REACH] = sums[d + REACH].astype(BF16)
                    t_copy(d).start()
                t_recv[REACH] = sums[REACH].astype(BF16)

    @pl.when(core == 0)
    def _():
        for d in steps:
            t_arrival(d).wait_recv()
        vertical(t_recv, rowed_ref)

    def part_arrival(k):
        remote(part_send.at[0], part_recv.at[k], part_s.at[0], part_r.at[k], (sibling, band)).wait_recv()

    @pl.when(core == 1)
    def _():
        @pl.when(jnp.logical_not(own_share))
        def _():
            part_arrival(0)

        for k in range(1, chips):
            part_arrival(k)
        for r in range(rank_count):
            total = part_recv[0, r].astype(F32)
            for k in range(1, chips):
                total = total + part_recv[k, r].astype(F32)
            rowed_ref[r] = total.astype(BF16)

    def p_copy(d):
        return remote(
            p_send.at[d + REACH], p_recv.at[d + REACH], p_s.at[d + REACH], p_r.at[d + REACH], frame_peer(-d)
        )

    rowed = [rowed_ref[r] for r in range(rank_count)]
    measured = None
    for d in steps + [0]:
        total = None
        for r in range(rank_count):
            term = dot(rowed[r], horiz[r, :, (d + REACH) * block : (d + REACH + 1) * block], ((1,), (1,)))
            total = term if total is None else total + term
        if d == 0:
            measured = total
        else:
            p_send[d + REACH] = total.astype(BF16)
            p_copy(d).start()
    for d in steps:
        p_copy(d).wait_recv()
        measured = measured + kept(p_recv[d + REACH].astype(F32), me + d, frame_devices)
    sensor_copy.wait()
    res_recv[REACH] = (measured - sensor_buf[...]).astype(BF16)

    def r_copy(d):
        return remote(
            res_recv.at[REACH], res_recv.at[d + REACH], r_s.at[d + REACH], r_r.at[d + REACH], frame_peer(d)
        )

    for d in steps:
        r_copy(d).start()
    for d in steps:
        r_copy(d).wait_recv()
    pieces = [kept(res_recv[d + REACH], me - d, frame_devices) for d in diagonals]
    for r in range(rank_count):
        total = None
        for d in diagonals:
            term = dot(pieces[d + REACH], horiz[r, :, (d + REACH) * block : (d + REACH + 1) * block], ((1,), (0,)))
            total = term if total is None else total + term
        spread[r] = total.astype(BF16)

    def q_copy(k):
        target = 2 * wrap(chip - k, chips) + lax.rem(chip, 2)
        return remote(spread, q_recv.at[k // 2], q_s.at[k], q_r.at[k // 2], (target, band))

    @pl.when(core == 1)
    def _():
        for k in [4, 5, 3, 6, 2, 7, 1]:
            q_copy(k).start()

        @pl.when(own_share)
        def _():
            q_recv[0] = spread[...]

        @pl.when(jnp.logical_not(own_share))
        def _():
            q_copy(0).start()

    def adjoint(tile_ref, store, keep):
        lhs = vert[...].reshape(rank_count * block, DIAGS * block)
        rhs = tile_ref[...].reshape(rank_count * block, slice_cols)
        products = dot(lhs, rhs, ((0,), (0,))).astype(BF16)
        for d in diagonals:
            target = keep if d == 0 else store
            target[d + REACH] = products[(d + REACH) * block : (d + REACH + 1) * block]

    def h_copy(d):
        return remote(
            h_send.at[d + REACH], h_recv.at[d + REACH], h_s.at[d + REACH], h_r.at[d + REACH], row_peer(d)
        )

    @pl.when(core == 0)
    def _():
        adjoint(spread, h_send, h_recv)
        for d in steps:
            h_copy(d).start()

    def hb_copy(i, d):
        return remote(
            hb_send.at[i, d + REACH], hb_recv.at[i, d + REACH], hb_s.at[i, d + REACH], hb_r.at[i, d + REACH], row_peer(d)
        )

    def gradient(sources_ref, frame, part):
        return weighted(
            [(sources_ref[d + REACH, part].astype(F32), on(frame, band - d)) for d in diagonals]
        ).astype(BF16)

    def g_copy(k):
        target = wrap(me + k, frame_devices)
        distance = wrap(target // 2 - chip, chips)
        return remote(
            g_send.at[target], grad_ref.at[:, :, columns(me)], g_s.at[k], g_r.at[distance], (target, band)
        )

    def give(q, carry):
        k = chips + ((q + 1) // 2) * (2 * lax.rem(q, 2) - 1)
        target = wrap(me + k, frame_devices)
        for f in range(local_count):
            g_send[target, f] = gradient(h_recv, target * local_count + f, slice(None))
        g_copy(k).start()
        return carry

    def q_arrival(i):
        remote(spread, q_recv.at[i], q_s.at[0], q_r.at[i], (sibling, band)).wait_recv()

    for position, i in enumerate([0, 3, 1, 2]):
        if i == 0:

            @pl.when(jnp.logical_not(own_share))
            def _():
                q_arrival(0)

        else:
            q_arrival(i)
        adjoint(q_recv.at[i], hb_send.at[i], hb_recv.at[i])
        for d in steps:
            hb_copy(i, d).start()
        if position == 1:

            @pl.when(core == 0)
            def _():
                for d in steps:
                    h_copy(d).wait_recv()
                lax.fori_loop(0, frame_devices - 1, give, 0)
                for f in range(local_count):
                    grad_ref[f, :, columns(me)] = gradient(h_recv, me * local_count + f, slice(None))

    def gb_copy(i):
        return remote(
            gb_send.at[i], grad_ref.at[:, :, columns(2 * odd_chip(i) + 1)], gb_s.at[i], gb_r.at[i], (sibling, band)
        )

    def gb_arrival(i):
        index = 2 * lax.rem(chip + 1 - skew + 2 * i, chips) + 1
        return remote(gb_send.at[i], grad_ref.at[:, :, columns(index)], gb_s.at[i], gb_r.at[i], (sibling, band))

    for i in [0, 3, 1, 2]:
        for d in steps:
            hb_copy(i, d).wait_recv()
        for f in range(local_count):
            gb_send[i, f] = gradient(hb_recv.at[i], sibling * local_count + f, slice(None))
        gb_copy(i).start()
        for f in range(local_count):
            grad_ref[f, :, columns(2 * odd_chip(i) + 1)] = gradient(
                hb_recv.at[i], me * local_count + f, slice(None)
            )

    def g_arrival(k):
        index = 2 * wrap(chip - k, chips)
        remote(g_send.at[0], grad_ref.at[:, :, columns(index)], g_s.at[0], g_r.at[k], (sibling, band)).wait_recv()

    for k in range(1, chips):
        g_arrival(k)

    @pl.when(core == 1)
    def _():
        g_arrival(0)
        even_copy(0).wait_send()
        for k in range(1, chips):
            q_copy(k).wait_send()

        @pl.when(jnp.logical_not(own_share))
        def _():
            q_copy(0).wait_send()

    @pl.when(core == 0)
    def _():
        def depart(k, carry):
            g_copy(k).wait_send()
            return carry

        lax.fori_loop(1, frame_devices, depart, 0)
        for d in steps:
            t_copy(d).wait_send()
            h_copy(d).wait_send()

    @pl.when(jnp.logical_not(own_share))
    def _():
        part_copy(0).wait_send()

    for k in range(1, chips):
        even_copy(k).wait_send()
    for i in range(shares):
        gb_arrival(i).wait_recv()
        gb_copy(i).wait_send()
        swap_copy(i).wait_send()
        if i > 0:
            part_copy(i).wait_send()
        for d in steps:
            tb_copy(i, d).wait_send()
            hb_copy(i, d).wait_send()
    for d in steps:
        p_copy(d).wait_send()
        r_copy(d).wait_send()


def per_device(
    video_frames, split_frames, dual_frames, sensor_image, kernel_vertical, kernel_horizontal, shutter_start, shutter_end
):
    local_count, block, width = video_frames.shape
    rank_count, taps = kernel_vertical.shape
    frame_devices = lax.axis_size("frame")
    slice_cols = width // frame_devices
    chips = frame_devices // 2
    shares = chips // 2
    hbm = pl.BlockSpec(memory_space=pltpu.HBM)
    dma = pltpu.SemaphoreType.DMA
    tile = (block, slice_cols)
    operands = (shutter_start, shutter_end, video_frames, sensor_image, kernel_vertical, kernel_horizontal)
    gradient = pl.pallas_call(
        kernel,
        out_shape=jax.ShapeDtypeStruct((local_count, block, width), BF16),
        in_specs=[hbm] * 6,
        out_specs=pl.BlockSpec(memory_space=pltpu.VMEM),
        scratch_shapes=[
            pltpu.SMEM(shutter_start.shape, jnp.int32),
            pltpu.SMEM(shutter_end.shape, jnp.int32),
            pltpu.VMEM((rank_count, taps), BF16),
            pltpu.VMEM((rank_count, taps), BF16),
            pltpu.VMEM(tile, F32),
            pltpu.VMEM((rank_count, block, taps + block), BF16),
            pltpu.VMEM((rank_count, block, taps + block), BF16),
            pltpu.VMEM((DIAGS,) + tile, F32),
        ]
        + [
            pltpu.VMEM(lead + tile, BF16)
            for lead in [
                (rank_count,), (rank_count,),
                (frame_devices, local_count), (shares, local_count), (shares, local_count),
                (shares, DIAGS), (shares, DIAGS), (shares, rank_count), (chips, rank_count),
                (DIAGS,), (DIAGS,), (DIAGS,), (DIAGS,), (DIAGS,), (DIAGS,), (DIAGS,),
                (shares, rank_count), (shares, DIAGS), (shares, DIAGS),
                (frame_devices, local_count), (shares, local_count),
            ]
        ]
        + [
            dma(count)
            for count in [
                (6,), (shares,), (shares,), (shares,), (chips,), (frame_devices,),
                (shares, DIAGS), (shares, DIAGS), (shares,), (chips,), (DIAGS,), (DIAGS,),
                (DIAGS,), (DIAGS,), (DIAGS,), (DIAGS,), (DIAGS,), (DIAGS,), (chips,), (shares,),
                (shares, DIAGS), (shares, DIAGS), (frame_devices,), (chips,), (shares,), (shares,),
            ]
        ],
        compiler_params=pltpu.CompilerParams(
            collective_id=0, has_side_effects=True, vmem_limit_bytes=32 << 20
        ),
        name="blur_and_adjoint",
    )(*[pltpu.with_memory_space_constraint(x, pltpu.HBM) for x in operands])
    current = video_frames.astype(F32)
    dual_value = dual_frames.astype(F32)
    moved_frames = current - tau_step * (
        gradient.astype(F32) + rho_weight * (current - split_frames.astype(F32) + dual_value)
    )
    shifted = moved_frames + dual_value
    clamped = jnp.maximum(shifted, 0.0)
    return (
        moved_frames.astype(BF16),
        clamped.astype(BF16),
        (shifted - clamped).astype(BF16),
    )


def solution(mesh):
    frames = P("frame", "row", None)
    return jax.shard_map(
        per_device,
        mesh=mesh,
        in_specs=(frames, frames, frames, P("row", None), P(), P(), P(), P()),
        out_specs=(frames, frames, frames),
        check_vma=False,
    )
```

time: 85.8 us -> 70.3 us (0.82)
  Pallas kernels: 82.1 us -> 66.8 us
    pallas_call x1, Pallas kernels: 82.1 us -> 66.8 us  [per_device(): pl.pallas_call(kernel, out_shape=jax.ShapeDtypeStruct((local_count, block...]
where the time goes in v3:
time: 70.3 us
  Pallas kernels  66.8 us (95%)
  other arithmetic  2.8 us (4%)
    pallas_call x1, Pallas kernels, per_device(): pl.pallas_call(kernel, out_shape=jax.ShapeDtypeStruct((local_count, block...  66.8 us
    convert_element_type x1, other arithmetic, per_device(): (shifted - clamped).astype(BF16)  2.8 us

profile of v3, /device:TPU:1, one launch (start us, length us, event | category | flops | bytes accessed | tf_op | source)
XLA Modules:
  0.0 70.3 jit_solution(15605848551677836651)
XLA Ops:
  0.6 0.0 copy-start
  0.6 0.0 copy-start.1
  0.7 0.0 copy-start.2
  0.7 66.8 %blur_and_adjoint.1 = bf16[2,128,2048]{2,1,0:T(8,128)(2,1)S(1)} custom-call(s32[16]{0:T(128)} %start_hbm.1, s32[16]{0:T(128)} %end_hbm.1, bf16[2,128,2048]{2,1,0:T(8,128)(2,1)} %video_ref.1, f32[128,2048]{1,0:T(8,128)} %sensor_ref.1, bf16[2,768]{1,0:T(2,128)(2,1)} %kv_hbm.1, bf16[2,768]{1,0:T(2,128)(2,1)} %kh_hbm.1), custom_call_target="tpu_custom_call" | custom-call | tf_op jit(solution)/shard_map/blur_and_adjoint/pallas_call | solution.py:489
  67.4 0.0 copy-done
  67.4 0.0 copy-done.1
  67.4 0.0 copy-done.2
  67.5 2.8 %fusion.3 = (bf16[2,128,2048]{2,1,0:T(8,128)(2,1)}, bf16[2,128,2048]{2,1,0:T(8,128)(2,1)}, bf16[2,128,2048]{2,1,0:T(8,128)(2,1)}) fusion(bf16[2,128,2048]{2,1,0:T(8,128)(2,1)S(1)} %copy-done.1, bf16[2,128,2048]{2,1,0:T(8,128)(2,1)S(1)} %copy-done.2, bf16[2,128,2048]{2,1,0:T(8,128)(2,1)S(1)} %blur_and_adjoint.1, bf16[2,128,2048]{2,1,0:T(8,128)(2,1)S(1)} %copy-done), kind=kLoop, calls=%fused_computation.9 | loop fusion | flops 8388608 | bytes 7340032 | tf_op jit(solution)/shard_map/convert_element_type | solution.py:539
Async XLA Ops:
  0.6 66.8 %copy-start = (bf16[2,128,2048]{2,1,0:T(8,128)(2,1)S(1)}, bf16[2,128,2048]{2,1,0:T(8,128)(2,1)}, u32[]{:S(2)}) copy-start(bf16[2,128,2048]{2,1,0:T(8,128)(2,1)} %video_ref.1) | copy-start | bytes 3145732
  0.6 66.8 %copy-start.1 = (bf16[2,128,2048]{2,1,0:T(8,128)(2,1)S(1)}, bf16[2,128,2048]{2,1,0:T(8,128)(2,1)}, u32[]{:S(2)}) copy-start(bf16[2,128,2048]{2,1,0:T(8,128)(2,1)} %param.10) | copy-start | bytes 3145732
  0.7 66.8 %copy-start.2 = (bf16[2,128,2048]{2,1,0:T(8,128)(2,1)S(1)}, bf16[2,128,2048]{2,1,0:T(8,128)(2,1)}, u32[]{:S(2)}) copy-start(bf16[2,128,2048]{2,1,0:T(8,128)(2,1)} %param.9) | copy-start | bytes 3145732

commit v4 on v3

--- a/solution.py
+++ b/solution.py
@@ -20,23 +20,32 @@
     return lax.dot_general(a, b, (contract, ((), ())), preferred_element_type=F32)
 
 
+def far_first(count):
+    return sorted(range(1, count), key=lambda k: -min(k, count - k))
+
+
 def wrap(index, count):
     return lax.rem(index + count, count)
 
 
-def banded(kernel_ref, out_ref, block):
+def banded(kernel_ref, scratch, block):
     rank_count, taps = kernel_ref.shape
     padded = jnp.concatenate(
         [kernel_ref[...].astype(F32), jnp.zeros((rank_count, block), F32)], axis=1
     )
     for r in range(rank_count):
         rows = jnp.broadcast_to(padded[r : r + 1], (block, taps + block))
-        out_ref[r] = pltpu.roll(rows, 0, 1, stride=1, stride_axis=0).astype(BF16)
+        scratch[r] = pltpu.roll(rows, 0, 1, stride=1, stride_axis=0)
+
+
+def spans(count, block):
+    return [slice(i * block, (i + 1) * block) for i in range(count)]
 
 
 def kernel(
-    start_hbm, end_hbm, video_ref, sensor_ref, kv_hbm, kh_hbm, grad_ref,
-    start_ref, end_ref, kv_ref, kh_ref, sensor_buf, vert, horiz, sums, rowed_ref, spread,
+    start_hbm, end_hbm, video_ref, sensor_ref, kv_hbm, kh_hbm, split_ref, dual_ref, grad_ref, base_ref,
+    video_buf, split_buf, dual_buf,
+    start_ref, end_ref, kv_ref, kh_ref, sensor_buf, bands_f32, vert, vert_t, horiz_p, horiz_q, sums, rowed_ref, spread,
     frames_buf, own_buf, swap_buf, tb_send, tb_recv, part_send, part_recv, t_send, t_recv,
     p_send, p_recv, res_recv, h_send, h_recv, q_recv, hb_send, hb_recv, g_send, gb_send,
     local_sem, own_sem, sw_s, sw_r, a_s, a_r, tb_s, tb_r, part_s, part_r, t_s, t_r,
@@ -53,7 +62,7 @@
     core = lax.rem(me, 2)
     sibling = me + 1 - 2 * core
     skew = lax.rem(core + chip, 2)
-    steps = [2, -2, 3, -3, 1, -1]
+    steps = [3, -3, 2, -2, 1, -1]
     diagonals = range(-REACH, REACH + 1)
 
     def frame_peer(d):
@@ -102,7 +111,8 @@
         pl.semaphore_signal(barrier, inc=1, device_id=frame_peer(k), device_id_type=MESH)
         return carry
 
-    lax.fori_loop(1, frame_devices, greet, 0)
+    for k in far_first(frame_devices):
+        greet(k, 0)
     for d in steps:
         pl.semaphore_signal(barrier, inc=1, device_id=row_peer(d), device_id_type=MESH)
     pl.semaphore_wait(barrier, frame_devices - 1 + len(steps))
@@ -121,20 +131,21 @@
     for i in order_b:
         swap_copy(i).start()
 
-    def start_even(k, carry):
+    for k in far_first(chips):
         even_copy(k).start()
-        return carry
-
-    lax.fori_loop(1, chips, start_even, 0)
 
     @pl.when(core == 1)
     def _():
         even_copy(0).start()
 
-    for copy in small:
+    loads = [
+        pltpu.make_async_copy(src, dst, local_sem.at[6 + i])
+        for i, (src, dst) in enumerate([(video_ref, video_buf), (split_ref, split_buf), (dual_ref, dual_buf)])
+    ]
+    for copy in loads:
+        copy.start()
+    for copy in small[:2]:
         copy.wait()
-    banded(kv_ref, vert, block)
-    banded(kh_ref, horiz, block)
 
     def on(frame, band_index):
         inside = (band_index >= 0) & (band_index < bands)
@@ -180,6 +191,34 @@
         for d in steps:
             tb_copy(i, d).start()
 
+    for copy in small[2:]:
+        copy.wait()
+    ranks = spans(rank_count, block)
+    blocks = spans(DIAGS, block)
+    banded(kv_ref, bands_f32, block)
+    for r in range(rank_count):
+        vert[ranks[r]] = bands_f32[r].astype(BF16)
+        for cols in blocks:
+            vert_t[cols, ranks[r]] = bands_f32[r, :, cols].T.astype(BF16)
+    banded(kh_ref, bands_f32, block)
+    for r in range(rank_count):
+        for cols in blocks:
+            horiz_p[ranks[r], cols] = bands_f32[r, :, cols].T.astype(BF16)
+            horiz_q[cols, ranks[r]] = bands_f32[r, :, cols].astype(BF16)
+
+    for copy in loads:
+        copy.wait()
+
+    def pull(c, carry):
+        part = pl.ds(pl.multiple_of(c * 16, 16), 16)
+        for f in range(local_count):
+            current = video_buf[f, part].astype(F32)
+            apart = current - split_buf[f, part].astype(F32) + dual_buf[f, part].astype(F32)
+            base_ref[f, part] = current - tau_step * rho_weight * apart
+        return carry
+
+    lax.fori_loop(0, block // 16, pull, 0)
+
     def add_frames(source, first):
         for d in diagonals:
             total = None if first else sums[d + REACH]
@@ -212,8 +251,9 @@
 
     def vertical(window_ref, store):
         window = jnp.concatenate([kept(window_ref[d + REACH], band + d, bands) for d in diagonals], axis=0)
+        products = dot(vert[...], window, ((1,), (0,))).astype(BF16)
         for r in range(rank_count):
-            store[r] = dot(vert[r], window, ((1,), (0,))).astype(BF16)
+            store[r] = products[ranks[r]]
 
     def part_copy(i):
         owner = 2 * odd_chip(i) + 1
@@ -283,18 +323,12 @@
             p_send.at[d + REACH], p_recv.at[d + REACH], p_s.at[d + REACH], p_r.at[d + REACH], frame_peer(-d)
         )
 
-    rowed = [rowed_ref[r] for r in range(rank_count)]
-    measured = None
-    for d in steps + [0]:
-        total = None
-        for r in range(rank_count):
-            term = dot(rowed[r], horiz[r, :, (d + REACH) * block : (d + REACH + 1) * block], ((1,), (1,)))
-            total = term if total is None else total + term
-        if d == 0:
-            measured = total
-        else:
-            p_send[d + REACH] = total.astype(BF16)
-            p_copy(d).start()
+    rowed = jnp.concatenate([rowed_ref[r] for r in range(rank_count)], axis=1)
+    products = dot(rowed, horiz_p[...], ((1,), (0,)))
+    for d in steps:
+        p_send[d + REACH] = products[:, blocks[d + REACH]].astype(BF16)
+        p_copy(d).start()
+    measured = products[:, blocks[REACH]]
     for d in steps:
         p_copy(d).wait_recv()
         measured = measured + kept(p_recv[d + REACH].astype(F32), me + d, frame_devices)
@@ -310,13 +344,10 @@
         r_copy(d).start()
     for d in steps:
         r_copy(d).wait_recv()
-    pieces = [kept(res_recv[d + REACH], me - d, frame_devices) for d in diagonals]
+    pieces = jnp.concatenate([kept(res_recv[d + REACH], me - d, frame_devices) for d in diagonals], axis=1)
+    products = dot(pieces, horiz_q[...], ((1,), (0,))).astype(BF16)
     for r in range(rank_count):
-        total = None
-        for d in diagonals:
-            term = dot(pieces[d + REACH], horiz[r, :, (d + REACH) * block : (d + REACH + 1) * block], ((1,), (0,)))
-            total = term if total is None else total + term
-        spread[r] = total.astype(BF16)
+        spread[r] = products[:, ranks[r]]
 
     def q_copy(k):
         target = 2 * wrap(chip - k, chips) + lax.rem(chip, 2)
@@ -336,12 +367,11 @@
             q_copy(0).start()
 
     def adjoint(tile_ref, store, keep):
-        lhs = vert[...].reshape(rank_count * block, DIAGS * block)
-        rhs = tile_ref[...].reshape(rank_count * block, slice_cols)
-        products = dot(lhs, rhs, ((0,), (0,))).astype(BF16)
+        tile = tile_ref[...].reshape(rank_count * block, slice_cols)
+        products = dot(vert_t[...], tile, ((1,), (0,))).astype(BF16)
         for d in diagonals:
             target = keep if d == 0 else store
-            target[d + REACH] = products[(d + REACH) * block : (d + REACH + 1) * block]
+            target[d + REACH] = products[blocks[d + REACH]]
 
     def h_copy(d):
         return remote(
@@ -394,7 +424,7 @@
         adjoint(q_recv.at[i], hb_send.at[i], hb_recv.at[i])
         for d in steps:
             hb_copy(i, d).start()
-        if position == 1:
+        if position == 0:
 
             @pl.when(core == 0)
             def _():
@@ -485,20 +515,24 @@
     hbm = pl.BlockSpec(memory_space=pltpu.HBM)
     dma = pltpu.SemaphoreType.DMA
     tile = (block, slice_cols)
-    operands = (shutter_start, shutter_end, video_frames, sensor_image, kernel_vertical, kernel_horizontal)
-    gradient = pl.pallas_call(
+    operands = (shutter_start, shutter_end, video_frames, sensor_image, kernel_vertical, kernel_horizontal, split_frames, dual_frames)
+    gradient, base = pl.pallas_call(
         kernel,
-        out_shape=jax.ShapeDtypeStruct((local_count, block, width), BF16),
-        in_specs=[hbm] * 6,
-        out_specs=pl.BlockSpec(memory_space=pltpu.VMEM),
-        scratch_shapes=[
+        out_shape=[jax.ShapeDtypeStruct((local_count, block, width), kind) for kind in (BF16, F32)],
+        in_specs=[hbm] * 8,
+        out_specs=[pl.BlockSpec(memory_space=pltpu.VMEM)] * 2,
+        scratch_shapes=[pltpu.VMEM((local_count, block, width), BF16)] * 3
+        + [
             pltpu.SMEM(shutter_start.shape, jnp.int32),
             pltpu.SMEM(shutter_end.shape, jnp.int32),
             pltpu.VMEM((rank_count, taps), BF16),
             pltpu.VMEM((rank_count, taps), BF16),
             pltpu.VMEM(tile, F32),
-            pltpu.VMEM((rank_count, block, taps + block), BF16),
-            pltpu.VMEM((rank_count, block, taps + block), BF16),
+            pltpu.VMEM((rank_count, block, taps + block), F32),
+            pltpu.VMEM((rank_count * block, taps + block), BF16),
+            pltpu.VMEM((taps + block, rank_count * block), BF16),
+            pltpu.VMEM((rank_count * block, taps + block), BF16),
+            pltpu.VMEM((taps + block, rank_count * block), BF16),
             pltpu.VMEM((DIAGS,) + tile, F32),
         ]
         + [
@@ -515,7 +549,7 @@
         + [
             dma(count)
             for count in [
-                (6,), (shares,), (shares,), (shares,), (chips,), (frame_devices,),
+                (9,), (shares,), (shares,), (shares,), (chips,), (frame_devices,),
                 (shares, DIAGS), (shares, DIAGS), (shares,), (chips,), (DIAGS,), (DIAGS,),
                 (DIAGS,), (DIAGS,), (DIAGS,), (DIAGS,), (DIAGS,), (DIAGS,), (chips,), (shares,),
                 (shares, DIAGS), (shares, DIAGS), (frame_devices,), (chips,), (shares,), (shares,),
@@ -526,12 +560,8 @@
         ),
         name="blur_and_adjoint",
     )(*[pltpu.with_memory_space_constraint(x, pltpu.HBM) for x in operands])
-    current = video_frames.astype(F32)
-    dual_value = dual_frames.astype(F32)
-    moved_frames = current - tau_step * (
-        gradient.astype(F32) + rho_weight * (current - split_frames.astype(F32) + dual_value)
-    )
-    shifted = moved_frames + dual_value
+    moved_frames = base - tau_step * gradient.astype(F32)
+    shifted = moved_frames + dual_frames.astype(F32)
     clamped = jnp.maximum(shifted, 0.0)
     return (
         moved_frames.astype(BF16),

time: 70.3 us -> 67.4 us (0.959)
  Pallas kernels: 66.8 us -> 64.4 us
    pallas_call x1, Pallas kernels: 66.8 us -> 64.4 us  [per_device(): pl.pallas_call(kernel, out_shape=[jax.ShapeDtypeStruct((local_count, bloc...]
where the time goes in v4:
time: 67.4 us
  Pallas kernels  64.4 us (96%)
  other arithmetic  2.32 us (3%)
    pallas_call x1, Pallas kernels, per_device(): pl.pallas_call(kernel, out_shape=[jax.ShapeDtypeStruct((local_count, bloc...  64.4 us
    convert_element_type x1, other arithmetic, per_device(): (shifted - clamped).astype(BF16)  2.32 us

profile of v4, /device:TPU:1, one launch (start us, length us, event | category | flops | bytes accessed | tf_op | source)
XLA Modules:
  0.0 67.4 jit_solution(8772973550556145800)
XLA Ops:
  0.6 0.0 copy-start
  0.6 64.4 %blur_and_adjoint.1 = (bf16[2,128,2048]{2,1,0:T(8,128)(2,1)S(1)}, f32[2,128,2048]{2,1,0:T(8,128)S(1)}) custom-call(s32[16]{0:T(128)} %start_hbm.1, s32[16]{0:T(128)} %end_hbm.1, bf16[2,128,2048]{2,1,0:T(8,128)(2,1)} %video_ref.1, f32[128,2048]{1,0:T(8,128)} %sensor_ref.1, bf16[2,768]{1,0:T(2,128)(2,1)} %kv_hbm.1, bf16[2,768]{1,0:T(2,128)(2,1)} %kh_hbm.1, ...), custom_call_target="tpu_custom_call" | custom-call | tf_op jit(solution)/shard_map/blur_and_adjoint/pallas_call | solution.py:519
  65.0 0.0 copy-done
  65.0 2.3 %fusion = (bf16[2,128,2048]{2,1,0:T(8,128)(2,1)}, bf16[2,128,2048]{2,1,0:T(8,128)(2,1)}, bf16[2,128,2048]{2,1,0:T(8,128)(2,1)}) fusion(bf16[2,128,2048]{2,1,0:T(8,128)(2,1)S(1)} %copy-done, f32[2,128,2048]{2,1,0:T(8,128)S(1)} %get-tuple-element.5, bf16[2,128,2048]{2,1,0:T(8,128)(2,1)S(1)} %get-tuple-element.6), kind=kLoop, calls=%fused_computation.2 | loop fusion | flops 5242880 | bytes 7340032 | tf_op jit(solution)/shard_map/convert_element_type | solution.py:569
Async XLA Ops:
  0.6 64.4 %copy-start = (bf16[2,128,2048]{2,1,0:T(8,128)(2,1)S(1)}, bf16[2,128,2048]{2,1,0:T(8,128)(2,1)}, u32[]{:S(2)}) copy-start(bf16[2,128,2048]{2,1,0:T(8,128)(2,1)} %dual_ref.1) | copy-start | bytes 3145732

commit v5 on v4

--- a/solution.py
+++ b/solution.py
@@ -355,9 +355,6 @@
 
     @pl.when(core == 1)
     def _():
-        for k in [4, 5, 3, 6, 2, 7, 1]:
-            q_copy(k).start()
-
         @pl.when(own_share)
         def _():
             q_recv[0] = spread[...]
@@ -365,6 +362,9 @@
         @pl.when(jnp.logical_not(own_share))
         def _():
             q_copy(0).start()
+
+        for k in [1, 7, 2, 6, 3, 5, 4]:
+            q_copy(k).start()
 
     def adjoint(tile_ref, store, keep):
         tile = tile_ref[...].reshape(rank_count * block, slice_cols)

time: 67.4 us -> 66.6 us (0.988)
  Pallas kernels: 64.4 us -> 63.5 us
    pallas_call x1, Pallas kernels: 64.4 us -> 63.5 us  [per_device(): pl.pallas_call(kernel, out_shape=[jax.ShapeDtypeStruct((local_count, bloc...]
where the time goes in v5:
time: 66.6 us; the launch traced here: 66.5 us
  Pallas kernels  63.5 us (95%)
  other arithmetic  2.32 us (3%)
    pallas_call x1, Pallas kernels, per_device(): pl.pallas_call(kernel, out_shape=[jax.ShapeDtypeStruct((local_count, bloc...  63.5 us
    convert_element_type x1, other arithmetic, per_device(): (shifted - clamped).astype(BF16)  2.32 us

profile of v5, /device:TPU:1, one launch (start us, length us, event | category | flops | bytes accessed | tf_op | source)
XLA Modules:
  0.0 66.5 jit_solution(5700536027502487655)
XLA Ops:
  0.6 0.0 copy-start
  0.6 63.5 %blur_and_adjoint.1 = (bf16[2,128,2048]{2,1,0:T(8,128)(2,1)S(1)}, f32[2,128,2048]{2,1,0:T(8,128)S(1)}) custom-call(s32[16]{0:T(128)} %start_hbm.1, s32[16]{0:T(128)} %end_hbm.1, bf16[2,128,2048]{2,1,0:T(8,128)(2,1)} %video_ref.1, f32[128,2048]{1,0:T(8,128)} %sensor_ref.1, bf16[2,768]{1,0:T(2,128)(2,1)} %kv_hbm.1, bf16[2,768]{1,0:T(2,128)(2,1)} %kh_hbm.1, ...), custom_call_target="tpu_custom_call" | custom-call | tf_op jit(solution)/shard_map/blur_and_adjoint/pallas_call | solution.py:519
  64.1 0.0 copy-done
  64.2 2.3 %fusion = (bf16[2,128,2048]{2,1,0:T(8,128)(2,1)}, bf16[2,128,2048]{2,1,0:T(8,128)(2,1)}, bf16[2,128,2048]{2,1,0:T(8,128)(2,1)}) fusion(bf16[2,128,2048]{2,1,0:T(8,128)(2,1)S(1)} %copy-done, f32[2,128,2048]{2,1,0:T(8,128)S(1)} %get-tuple-element.5, bf16[2,128,2048]{2,1,0:T(8,128)(2,1)S(1)} %get-tuple-element.6), kind=kLoop, calls=%fused_computation.2 | loop fusion | flops 5242880 | bytes 7340032 | tf_op jit(solution)/shard_map/convert_element_type | solution.py:569
Async XLA Ops:
  0.6 63.5 %copy-start = (bf16[2,128,2048]{2,1,0:T(8,128)(2,1)S(1)}, bf16[2,128,2048]{2,1,0:T(8,128)(2,1)}, u32[]{:S(2)}) copy-start(bf16[2,128,2048]{2,1,0:T(8,128)(2,1)} %dual_ref.1) | copy-start | bytes 3145732

commit v6 on v5

--- a/solution.py
+++ b/solution.py
@@ -329,11 +329,12 @@
         p_send[d + REACH] = products[:, blocks[d + REACH]].astype(BF16)
         p_copy(d).start()
     measured = products[:, blocks[REACH]]
-    for d in steps:
+    sensor_copy.wait()
+    measured = measured - sensor_buf[...]
+    for d in reversed(steps):
         p_copy(d).wait_recv()
         measured = measured + kept(p_recv[d + REACH].astype(F32), me + d, frame_devices)
-    sensor_copy.wait()
-    res_recv[REACH] = (measured - sensor_buf[...]).astype(BF16)
+    res_recv[REACH] = measured.astype(BF16)
 
     def r_copy(d):
         return remote(

time: 66.6 us -> 66.6 us (level)
  no operation moved by 1% of the time
where the time goes in v6:
time: 66.6 us; the launch traced here: 66.5 us
  Pallas kernels  63.5 us (95%)
  other arithmetic  2.32 us (3%)
    pallas_call x1, Pallas kernels, per_device(): pl.pallas_call(kernel, out_shape=[jax.ShapeDtypeStruct((local_count, bloc...  63.5 us
    convert_element_type x1, other arithmetic, per_device(): (shifted - clamped).astype(BF16)  2.32 us

profile of v6, /device:TPU:1, one launch (start us, length us, event | category | flops | bytes accessed | tf_op | source)
XLA Modules:
  0.0 66.5 jit_solution(9653489632427534187)
XLA Ops:
  0.6 0.0 copy-start
  0.6 63.5 %blur_and_adjoint.1 = (bf16[2,128,2048]{2,1,0:T(8,128)(2,1)S(1)}, f32[2,128,2048]{2,1,0:T(8,128)S(1)}) custom-call(s32[16]{0:T(128)} %start_hbm.1, s32[16]{0:T(128)} %end_hbm.1, bf16[2,128,2048]{2,1,0:T(8,128)(2,1)} %video_ref.1, f32[128,2048]{1,0:T(8,128)} %sensor_ref.1, bf16[2,768]{1,0:T(2,128)(2,1)} %kv_hbm.1, bf16[2,768]{1,0:T(2,128)(2,1)} %kh_hbm.1, ...), custom_call_target="tpu_custom_call" | custom-call | tf_op jit(solution)/shard_map/blur_and_adjoint/pallas_call | solution.py:520
  64.2 0.0 copy-done
  64.2 2.3 %fusion = (bf16[2,128,2048]{2,1,0:T(8,128)(2,1)}, bf16[2,128,2048]{2,1,0:T(8,128)(2,1)}, bf16[2,128,2048]{2,1,0:T(8,128)(2,1)}) fusion(bf16[2,128,2048]{2,1,0:T(8,128)(2,1)S(1)} %copy-done, f32[2,128,2048]{2,1,0:T(8,128)S(1)} %get-tuple-element.5, bf16[2,128,2048]{2,1,0:T(8,128)(2,1)S(1)} %get-tuple-element.6), kind=kLoop, calls=%fused_computation.2 | loop fusion | flops 5242880 | bytes 7340032 | tf_op jit(solution)/shard_map/convert_element_type | solution.py:570
Async XLA Ops:
  0.6 63.6 %copy-start = (bf16[2,128,2048]{2,1,0:T(8,128)(2,1)S(1)}, bf16[2,128,2048]{2,1,0:T(8,128)(2,1)}, u32[]{:S(2)}) copy-start(bf16[2,128,2048]{2,1,0:T(8,128)(2,1)} %dual_ref.1) | copy-start | bytes 3145732
